TPU v7x, 512 devices: a whole 4x4x16 slice. The times are simulated.
512 devices in a mesh: gx: 32 (over z, x_lo), gy: 16 (over x_hi, y, core).
Axes of the slice: x: 4 (x_hi: 2, x_lo: 2; x = x_hi * 2 + x_lo), y: 4, z: 16, core: 2. Of those that a mesh axis runs over, the one named last changes fastest.
Arguments:
- positions: float32 [32, 16, 3, 128], P('gx', 'gy'), may hold values from 0 to 29
- species: int32 [32, 16, 128], P('gx', 'gy'), may hold values from 0 to 4
- senders: int32 [32, 16, 3, 128], P('gx', 'gy'), may hold values from 0 to 639, as said below
- counts: int32 [32, 16, 128], P('gx', 'gy'), may hold values from 1 to 3, as said below
- owners: int32 [32, 16, 3, 128], P('gx', 'gy'), may hold values 0 or 1
- send_list: int32 [32, 16, 64], P('gx', 'gy'), may hold values from 0 to 127, as said below
- embedding: float32 [128, 5], replicated, may hold values from -6 to 6
- radial_in_one: float32 [64, 8], replicated, may hold values from -2 to 2
- radial_mid_one: float32 [64, 64], replicated, may hold values from -0.75 to 0.75
- radial_out_one: float32 [384, 64], replicated, may hold values from -0.75 to 0.75
- mixing: float32 [3, 128, 128], replicated, may hold values from -0.5 to 0.5
- square_mix: float32 [128, 128], replicated, may hold values from -0.5 to 0.5
- readout_one: float32 [128], replicated, may hold values from -0.5 to 0.5
- radial_in_two: float32 [64, 8], replicated, may hold values from -2 to 2
- radial_mid_two: float32 [64, 64], replicated, may hold values from -0.75 to 0.75
- radial_out_two: float32 [384, 64], replicated, may hold values from -0.75 to 0.75
- mix_two: float32 [128, 128], replicated, may hold values from -0.5 to 0.5
- read_hidden: float32 [16, 128], replicated, may hold values from -0.5 to 0.5
- read_out: float32 [16], replicated, may hold values from -1.5 to 1.5
Outputs:
- forces: float32 [32, 16, 3, 128], P('gx', 'gy')
- energies: float32 [32, 16, 128], P('gx', 'gy')
Inputs may be any that keep to these rules, and one draw needn't show every extreme that they name: `counts`: every atom has at least one live slot, and some atom of every domain has all 3 slots live. `send_list`: each domain's list holds 64 distinct atoms of that domain. `senders`: an atom's slots name distinct atoms other than itself. Atom n of a domain sits at lattice site ((n // 2) // 8, (n // 2) % 8, n % 2); a ghost taken from the domain at offset (i - 1, j - 1) sits at its own site in that domain plus ((i - 1) * 8, (j - 1) * 8, 0). The site of every atom that a slot names differs from the site of the slot's atom by at most one along each of the three dimensions.
All inputs are finite; a program needn't handle non-finite values. No bound on the sum of `owners` on one device may be relied on, other than what follows from the above.
Results may differ from a plain program's by a relative error of at most 0.0003.
Values sent between devices are 32-bit elements; how exact they have to be, the bound alone decides.
No kernel may reach another device: no remote copies, remote signals or barrier semaphores. Data moves between devices by JAX's collectives and lax.ppermute only.
A program may use at most 64 MiB of HBM per device.

v0:
```python
import math

import jax
import jax.numpy as jnp
from jax import lax
from jax.sharding import PartitionSpec as P

SIDE = 8


precise = lax.Precision.HIGHEST
spacing = 1.75
cutoff = 5.0
soften = 0.25
pair_strength = 2.0


def from_behind(value, axis, steps):
    count = lax.axis_size(axis)
    pairs = [(source, (source + steps) % count) for source in range(count)]
    return lax.ppermute(value, axis, pairs)


def extended(cells, sides, width):
    for axis, dim in sides:
        count = lax.axis_size(axis)
        head = lax.slice_in_dim(cells, 0, width, axis=dim)
        tail = lax.slice_in_dim(cells, cells.shape[dim] - width, cells.shape[dim], axis=dim)
        cells = jnp.concatenate(
            [
                lax.ppermute(tail, axis, [(i, (i + 1) % count) for i in range(count)]),
                cells,
                lax.ppermute(head, axis, [((i + 1) % count, i) for i in range(count)]),
            ],
            axis=dim,
        )
    return cells


def product(left_side, right_side):
    return jnp.dot(left_side, right_side, precision=precise, preferred_element_type=jnp.float32)


def harmonics(direction):
    along_x = direction[0]
    along_y = direction[1]
    along_z = direction[2]
    root_three = math.sqrt(3.0)
    root_five = math.sqrt(5.0)
    root_fifteen = math.sqrt(15.0)
    return jnp.stack(
        [
            jnp.ones_like(along_x),
            root_three * along_x,
            root_three * along_y,
            root_three * along_z,
            root_fifteen * along_x * along_y,
            root_fifteen * along_y * along_z,
            0.5 * root_five * (2.0 * along_z * along_z - along_x * along_x - along_y * along_y),
            root_fifteen * along_x * along_z,
            0.5 * root_fifteen * (along_x * along_x - along_y * along_y),
        ]
    )


def geometry(places, ghost_places, table_index, basis_count):
    places_all = jnp.concatenate([places, ghost_places], axis=1)
    repeats = table_index.shape[0] // places.shape[1]
    displace = places_all[:, table_index] - jnp.tile(places, (1, repeats))
    radius = jnp.sqrt(jnp.sum(displace * displace, axis=0) + soften)
    direction = displace / radius
    scaled_radius = jnp.minimum(radius / cutoff, 1.0)
    envelope = 1.0 - 28.0 * scaled_radius**6 + 48.0 * scaled_radius**7 - 21.0 * scaled_radius**8
    orders = jnp.arange(1, basis_count + 1).astype(jnp.float32)[:, None]
    radial_basis = (
        math.sqrt(2.0 / cutoff) * jnp.sin(orders * math.pi * scaled_radius) / radius * envelope
    )
    return (harmonics(direction), radial_basis, envelope, radius)


def radial(radial_basis, weight_in, weight_mid, weight_out):
    hidden = jax.nn.silu(product(weight_in, radial_basis))
    hidden = jax.nn.silu(product(weight_mid, hidden))
    return product(weight_out, hidden)


def flat_index(senders, atom_count, bound_count):
    ghost_slot = senders - atom_count
    blocks_of = ghost_slot // bound_count
    blocks_of = blocks_of + (blocks_of >= 4).astype(jnp.int32)
    spot = atom_count + blocks_of * bound_count + ghost_slot % bound_count
    return jnp.where(senders < atom_count, senders, spot).reshape(-1)


def live_slots(counts, slot_count):
    return (jnp.arange(slot_count)[:, None] < counts[None, :]).astype(jnp.float32).reshape(-1)


def ghost_shift(bound_count):
    blocks_of = jnp.arange(9 * bound_count) // bound_count
    side_length = spacing * SIDE
    shift_x = (blocks_of // 3 - 1).astype(jnp.float32) * side_length
    shift_y = (blocks_of % 3 - 1).astype(jnp.float32) * side_length
    return jnp.stack([shift_x, shift_y, jnp.zeros_like(shift_x)])


def lookup(embedding, element_codes):
    one_hot = (jnp.arange(embedding.shape[1])[:, None] == element_codes[None, :]).astype(
        jnp.float32
    )
    return product(embedding, one_hot)


def blocks_to_table(arrived):
    rows_each = arrived.shape[2]
    stacked = arrived.reshape(9, rows_each, arrived.shape[3])
    return jnp.moveaxis(stacked, 0, 1).reshape(rows_each, -1)


def layer_one(
    places,
    ghost_places,
    embedded,
    ghost_embedded,
    table_index,
    live_mask,
    owner_mask,
    weight_in,
    weight_mid,
    weight_out,
    mixing,
    square_mix,
    readout_one,
):
    shapes, radial_basis, envelope, radius = geometry(
        places, ghost_places, table_index, weight_in.shape[1]
    )
    atom_count = places.shape[1]
    channels = embedded.shape[0]
    slot_count = table_index.shape[0] // atom_count
    edge_weight = radial(radial_basis, weight_in, weight_mid, weight_out).reshape(3, channels, -1)
    sender_rows = jnp.concatenate([embedded, ghost_embedded], axis=1)[:, table_index]
    carried = (edge_weight * (sender_rows * live_mask)[None]).reshape(
        3, channels, slot_count, atom_count
    )
    shaped = shapes.reshape(9, slot_count, atom_count)
    scalar_part = jnp.einsum("cna,na->ca", carried[0], shaped[0], precision=precise)[None]
    vector_part = jnp.einsum("cna,kna->kca", carried[1], shaped[1:4], precision=precise)
    tensor_part = jnp.einsum("cna,kna->kca", carried[2], shaped[4:9], precision=precise)
    moments = jnp.concatenate([scalar_part, vector_part, tensor_part], 0) / slot_count
    squares = jnp.sum(moments * moments, axis=0)
    scalar_feature = product(mixing[0], moments[0]) + product(square_mix, squares) + embedded
    vectors = jnp.einsum("ij,kja->kia", mixing[1], moments[1:4], precision=precise)
    tensors = jnp.einsum("ij,kja->kia", mixing[2], moments[4:9], precision=precise)
    features = jnp.concatenate([scalar_feature[None], vectors, tensors], 0).reshape(
        9 * channels, atom_count
    )
    pair_energy = (
        (owner_mask * live_mask * pair_strength * jnp.exp(-radius) * envelope)
        .reshape(slot_count, atom_count)
        .sum(0)
    )
    energy = product(readout_one, scalar_feature) + pair_energy
    return (features, energy)


def layer_two(
    places,
    ghost_places,
    features,
    ghost_features,
    table_index,
    live_mask,
    weight_in,
    weight_mid,
    weight_out,
    mix_two,
    read_hidden,
    read_out,
):
    shapes, radial_basis, envelope, radius = geometry(
        places, ghost_places, table_index, weight_in.shape[1]
    )
    atom_count = places.shape[1]
    channels = mix_two.shape[0]
    slot_count = table_index.shape[0] // atom_count
    edge_weight = radial(radial_basis, weight_in, weight_mid, weight_out).reshape(3, channels, -1)
    sender_rows = jnp.concatenate([features, ghost_features], axis=1)[:, table_index].reshape(
        9, channels, -1
    )
    projected = sender_rows * shapes[:, None, :]
    scalar = (
        edge_weight[0] * projected[0]
        + edge_weight[1] * jnp.sum(projected[1:4], 0)
        + edge_weight[2] * jnp.sum(projected[4:9], 0)
    ) * live_mask
    gathered = scalar.reshape(channels, slot_count, atom_count).sum(1) / slot_count
    refined = product(mix_two, gathered) + features[:channels]
    return product(read_out, jax.nn.silu(product(read_hidden, refined)))


def send_back(ghost_grad, bound_count):
    rows_each = ghost_grad.shape[0]
    pieces = ghost_grad.reshape(rows_each, 3, 3, bound_count)
    from_lower = from_behind(pieces[:, 2], "gx", 1)
    from_upper = from_behind(pieces[:, 0], "gx", -1)
    merged = pieces[:, 1] + from_lower + from_upper
    from_below = from_behind(merged[:, 2], "gy", 1)
    from_above = from_behind(merged[:, 0], "gy", -1)
    return merged[:, 1] + from_below + from_above


def local(
    positions,
    species,
    senders,
    counts,
    owners,
    send_list,
    embedding,
    radial_in_one,
    radial_mid_one,
    radial_out_one,
    mixing,
    square_mix,
    readout_one,
    radial_in_two,
    radial_mid_two,
    radial_out_two,
    mix_two,
    read_hidden,
    read_out,
):
    places = positions[0, 0]
    species_here = species[0, 0]
    outgoing = send_list[0, 0]
    atom_count = places.shape[1]
    bound_count = outgoing.shape[0]
    table_index = flat_index(senders[0, 0], atom_count, bound_count)
    live_mask = live_slots(counts[0, 0], senders.shape[2])
    owner_mask = owners[0, 0].astype(jnp.float32).reshape(-1)
    embedded = lookup(embedding, species_here)
    bound_places = places[:, outgoing]
    code_rows = species_here[outgoing].astype(jnp.float32)[None]
    outbound = jnp.concatenate([bound_places, code_rows], 0)
    arrived = extended(outbound[None, None], (("gx", 0), ("gy", 1)), 1)
    spread = blocks_to_table(arrived)
    ghost_places = spread[:3]
    ghost_embedded = lookup(embedding, spread[3].astype(jnp.int32))
    ghost_places = ghost_places + ghost_shift(bound_count)

    def first_layer(place_arg, ghost_arg):
        return layer_one(
            place_arg,
            ghost_arg,
            embedded,
            ghost_embedded,
            table_index,
            live_mask,
            owner_mask,
            radial_in_one,
            radial_mid_one,
            radial_out_one,
            mixing,
            square_mix,
            readout_one,
        )

    outputs_one, pullback_one = jax.vjp(first_layer, places, ghost_places)
    features, energy_one = outputs_one
    outbound_two = features[:, outgoing][None, None]
    arrived_two = extended(outbound_two, (("gx", 0), ("gy", 1)), 1)
    ghost_features = blocks_to_table(arrived_two)

    def second_layer(place_arg, ghost_arg, feature_arg, ghost_feature_arg):
        return layer_two(
            place_arg,
            ghost_arg,
            feature_arg,
            ghost_feature_arg,
            table_index,
            live_mask,
            radial_in_two,
            radial_mid_two,
            radial_out_two,
            mix_two,
            read_hidden,
            read_out,
        )

    energy_two, pullback_two = jax.vjp(second_layer, places, ghost_places, features, ghost_features)
    grad_places, grad_ghosts, grad_features, grad_ghost_features = pullback_two(
        jnp.ones_like(energy_two)
    )
    returned = send_back(jnp.concatenate([grad_ghost_features, grad_ghosts], 0), bound_count)
    feature_back = returned[:-3]
    place_back_two = returned[-3:]
    grad_features = grad_features.at[:, outgoing].add(feature_back)
    grad_first, grad_ghost_first = pullback_one((grad_features, jnp.ones_like(energy_one)))
    place_back = send_back(grad_ghost_first, bound_count) + place_back_two
    grad_total = (grad_places + grad_first).at[:, outgoing].add(place_back)
    return ((-grad_total)[None, None], (energy_one + energy_two)[None, None])


def solution(mesh):
    placed = (
        P("gx", "gy", None, None),
        P("gx", "gy", None),
        P("gx", "gy", None, None),
        P("gx", "gy", None),
        P("gx", "gy", None, None),
        P("gx", "gy", None),
        P(),
        P(),
        P(),
        P(),
        P(),
        P(),
        P(),
        P(),
        P(),
        P(),
        P(),
        P(),
        P(),
    )
    return jax.shard_map(
        local,
        mesh=mesh,
        in_specs=placed,
        out_specs=(P("gx", "gy", None, None), P("gx", "gy", None)),
        check_vma=False,
    )
```

profile of v0, /device:TPU:25, one launch (start us, length us, event | category | flops | bytes accessed | tf_op | source)
XLA Modules:
  0.0 230.0 jit_solution(4839749614853817997)
XLA Ops:
  4.3 12.1 %collective-permute-start.1 = (f32[1,1,4,64]{3,2,1,0:T(4,128)S(1)}, f32[1,1,4,64]{3,2,1,0:T(4,128)S(1)}, u32[]{:S(2)}, u32[]{:S(2)}) collective-permute-start(f32[1,1,4,64]{3,2,1,0:T(4,128)S(1)} %maximum_bitcast_fusion), channel_id=1, source_target_pairs={{16,0},{32,16},{48,32},{64,48},{80,64},{96,80},{112,96},{128,112},... | collective-permute-start | bytes 3080 | tf_op jit(solution)/shard_map/ppermute | solution.py:33
  16.4 1.9 collective-permute-start
  20.7 2.1 collective-permute-done
  22.8 4.0 %collective-permute-start.3 = (f32[3,1,4,64]{3,2,1,0:T(4,128)S(1)}, f32[3,1,4,64]{3,2,1,0:T(4,128)S(1)}, u32[]{:S(2)}, u32[]{:S(2)}) collective-permute-start(f32[3,1,4,64]{3,2,1,0:T(4,128)S(1)} %pad_maximum_fusion.9), channel_id=1, source_target_pairs={{1,0},{2,1},{3,2},{4,3},{5,4},{6,5},{7,6},{8,7},{9,8},{10,9},{11,1... | collective-permute-start | bytes 9224 | tf_op jit(solution)/shard_map/ppermute | solution.py:33
  26.8 5.2 %collective-permute-start.2 = (f32[3,1,4,64]{3,2,1,0:T(4,128)S(1)}, f32[3,1,4,64]{3,2,1,0:T(4,128)S(1)}, u32[]{:S(2)}, u32[]{:S(2)}) collective-permute-start(f32[3,1,4,64]{3,2,1,0:T(4,128)S(1)} %pad_maximum_fusion.9), channel_id=1, source_target_pairs={{0,1},{1,2},{2,3},{3,4},{4,5},{5,6},{6,7},{7,8},{8,9},{9,10},{10,1... | collective-permute-start | bytes 9224 | tf_op jit(solution)/shard_map/ppermute | solution.py:31
  48.1 3.4 %collective-permute-start.5 = (f32[1,1,1152,64]{2,3,1,0:T(8,128)S(1)}, f32[1,1,1152,64]{2,3,1,0:T(8,128)S(1)}, u32[]{:S(2)}, u32[]{:S(2)}) collective-permute-start(f32[1,1,1152,64]{2,3,1,0:T(8,128)S(1)} %bitcast.399), channel_id=1, source_target_pairs={{16,0},{32,16},{48,32},{64,48},{80,64},{96,80},{112,96},{128,112},... | collective-permute-start | bytes 884744 | tf_op jit(solution)/shard_map/ppermute | solution.py:33
  51.5 1.9 collective-permute-start.4
  53.5 11.1 %collective-permute-done.5 = f32[1,1,1152,64]{2,3,1,0:T(8,128)S(1)} collective-permute-done((f32[1,1,1152,64]{2,3,1,0:T(8,128)S(1)}, f32[1,1,1152,64]{2,3,1,0:T(8,128)S(1)}, u32[]{:S(2)}, u32[]{:S(2)}) %collective-permute-start.5) | collective-permute-done | bytes 294944 | tf_op jit(solution)/shard_map/ppermute | solution.py:33
  64.6 2.1 collective-permute-start.7
  66.7 7.3 %collective-permute-start.6 = (f32[3,1,1152,64]{2,3,1,0:T(8,128)S(1)}, f32[3,1,1152,64]{2,3,1,0:T(8,128)}, u32[]{:S(2)}, u32[]{:S(2)}) collective-permute-start(f32[3,1,1152,64]{2,3,1,0:T(8,128)S(1)} %pad_maximum_fusion.4), channel_id=1, source_target_pairs={{0,1},{1,2},{2,3},{3,4},{4,5},{5,6},{6,7},{7,8},{8,9},{9,10},{10,1... | collective-permute-start | bytes 2654216 | tf_op jit(solution)/shard_map/ppermute | solution.py:31
  77.4 5.2 %collective-permute-done.7 = f32[3,1,1152,64]{2,3,1,0:T(8,128)S(1)} collective-permute-done((f32[3,1,1152,64]{2,3,1,0:T(8,128)S(1)}, f32[3,1,1152,64]{2,3,1,0:T(8,128)S(1)}, u32[]{:S(2)}, u32[]{:S(2)}) %collective-permute-start.7) | collective-permute-done | bytes 884768 | tf_op jit(solution)/shard_map/ppermute | solution.py:33
  85.4 2.8 %gather_fusion.5 = f32[384,1152]{1,0:T(8,128)} fusion(f32[1152,704]{0,1:T(8,128)S(1)} %pad_maximum_fusion, s32[1024]{0:T(1024)} %copy-done.50), kind=kCustom, calls=%fused_computation.5 | custom fusion | bytes 3540480 | tf_op jit(solution)/shard_map/jvp()/gather | solution.py:188
  88.2 2.2 copy.489
  104.4 1.9 copy.496
  107.4 2.1 scatter_custom_fusion
  111.0 5.9 %scatter_custom_fusion.1 = f32[1152,704]{0,1:T(8,128)S(1)} fusion(s32[384]{0:T(512)} %copy-done.57, f32[1152,384]{0,1:T(8,128)} %copy.496, f32[]{:T(128)} %constant.112.clone.1), kind=kCustom, calls=%fused_computation.14 | custom fusion | flops 442368 | bytes 5014016 | tf_op jit(solution)/shard_map/transpose(jvp())/scatter-add | solution.py:188
  121.1 1.9 collective-permute-start.8
  123.1 5.5 %collective-permute-start.9 = (f32[1155,3,64]{0,2,1:T(8,128)}, f32[1155,3,64]{0,2,1:T(8,128)}, u32[]{:S(2)}, u32[]{:S(2)}) collective-permute-start(f32[1155,3,64]{0,2,1:T(8,128)} %get-tuple-element.31), channel_id=1, source_target_pairs={{0,496},{16,0},{32,16},{48,32},{64,48},{80,64},{96,80},{112,96},{1... | collective-permute-start | bytes 2661128 | tf_op jit(solution)/shard_map/ppermute | solution.py:21
  129.7 1.7 copy.525
  133.8 29.8 %collective-permute-done.8 = f32[1155,3,64]{0,2,1:T(8,128)} collective-permute-done((f32[1155,3,64]{0,2,1:T(8,128)}, f32[1155,3,64]{0,2,1:T(8,128)}, u32[]{:S(2)}, u32[]{:S(2)}) %collective-permute-start.8) | collective-permute-done | bytes 887072 | tf_op jit(solution)/shard_map/ppermute | solution.py:21
  163.6 4.1 %collective-permute-done.9 = f32[1155,3,64]{0,2,1:T(8,128)} collective-permute-done((f32[1155,3,64]{0,2,1:T(8,128)}, f32[1155,3,64]{0,2,1:T(8,128)}, u32[]{:S(2)}, u32[]{:S(2)}) %collective-permute-start.9) | collective-permute-done | bytes 887072 | tf_op jit(solution)/shard_map/ppermute | solution.py:21
  167.7 1.9 fusion.14
  169.7 3.8 %collective-permute-start.10 = (f32[1155,64]{0,1:T(8,128)S(1)}, f32[1155,64]{0,1:T(8,128)S(1)}, u32[]{:S(2)}, u32[]{:S(2)}) collective-permute-start(f32[1155,64]{0,1:T(8,128)S(1)} %get-tuple-element.34), channel_id=1, source_target_pairs={{0,1},{1,2},{2,3},{3,4},{4,5},{5,6},{6,7},{7,8},{8,9},{9,10},{10,1... | collective-permute-start | bytes 887048 | tf_op jit(solution)/shard_map/ppermute | solution.py:21
  173.6 1.9 collective-permute-start.11
  177.6 8.0 %collective-permute-done.11 = f32[1155,64]{0,1:T(8,128)S(1)} collective-permute-done((f32[1155,64]{0,1:T(8,128)S(1)}, f32[1155,64]{0,1:T(8,128)S(1)}, u32[]{:S(2)}, u32[]{:S(2)}) %collective-permute-start.11) | collective-permute-done | bytes 295712 | tf_op jit(solution)/shard_map/ppermute | solution.py:21
  185.6 3.1 %scatter_custom_fusion.2 = f32[1152,128]{0,1:T(8,128)} fusion(f32[1152,128]{0,1:T(8,128)} %slice_add_fusion, s32[64]{0:T(128)} %copy-done.70, f32[1155,64]{0,1:T(8,128)S(1)} %fusion.19), kind=kCustom, calls=%fused_computation.88 | custom fusion | flops 73728 | bytes 884736 | tf_op jit(solution)/shard_map/scatter-add | solution.py:298
  205.3 2.1 scatter_custom_fusion.3
  207.5 1.9 collective-permute-start.12
  209.4 5.5 %collective-permute-start.13 = (f32[3,3,64]{0,2,1:T(8,128)S(1)}, f32[3,3,64]{0,2,1:T(8,128)S(1)}, u32[]{:S(2)}, u32[]{:S(2)}) collective-permute-start(f32[3,3,64]{0,2,1:T(8,128)S(1)} %get-tuple-element.45), channel_id=1, source_target_pairs={{0,496},{16,0},{32,16},{48,32},{64,48},{80,64},{96,80},{112,96},{1... | collective-permute-start | bytes 6920 | tf_op jit(solution)/shard_map/ppermute | solution.py:21
  216.5 2.9 %collective-permute-start.14 = (f32[3,64]{0,1:T(8,128)S(1)}, f32[3,64]{0,1:T(8,128)S(1)}, u32[]{:S(2)}, u32[]{:S(2)}) collective-permute-start(f32[3,64]{0,1:T(8,128)S(1)} %get-tuple-element.49), channel_id=1, source_target_pairs={{0,1},{1,2},{2,3},{3,4},{4,5},{5,6},{6,7},{7,8},{8,9},{9,10},{10,1... | collective-permute-start | bytes 2312 | tf_op jit(solution)/shard_map/ppermute | solution.py:21
  219.4 1.9 collective-permute-start.15
  221.5 6.8 %collective-permute-done.15 = f32[3,64]{0,1:T(8,128)S(1)} collective-permute-done((f32[3,64]{0,1:T(8,128)S(1)}, f32[3,64]{0,1:T(8,128)S(1)}, u32[]{:S(2)}, u32[]{:S(2)}) %collective-permute-start.15) | collective-permute-done | bytes 800 | tf_op jit(solution)/shard_map/ppermute | solution.py:21
  (347 shorter events, 73.3 us)
Async XLA Ops:
  0.6 75.3 %copy-start = (f32[384,64]{0,1:T(8,128)S(1)}, f32[384,64]{0,1:T(8,128)}, u32[]{:S(2)}) copy-start(f32[384,64]{0,1:T(8,128)} %param.34) | copy-start | bytes 294916
  0.6 37.2 %copy-start.76 = (f32[64,8]{0,1:T(8,128)S(1)}, f32[64,8]{0,1:T(8,128)}, u32[]{:S(2)}) copy-start(f32[64,8]{0,1:T(8,128)} %param.26) | copy-start | bytes 6148
  0.7 37.6 %copy-start.72 = (f32[64,64]{1,0:T(8,128)S(1)}, f32[64,64]{1,0:T(8,128)}, u32[]{:S(2)}) copy-start(f32[64,64]{1,0:T(8,128)} %param.27) | copy-start | bytes 49156
  1.4 31.4 %copy-start.70 = (s32[64]{0:T(128)}, s32[64]{0:T(128)S(1)}, u32[]{:S(2)}) copy-start(s32[64]{0:T(128)S(1)} %fusion.175) | copy-start | bytes 772
  3.5 35.0 %copy-start.31 = (f32[384,64]{0,1:T(8,128)S(1)}, f32[384,64]{0,1:T(8,128)}, u32[]{:S(2)}) copy-start(f32[384,64]{0,1:T(8,128)} %param.28) | copy-start | bytes 294916
  4.3 16.4 %collective-permute-start.1 = (f32[1,1,4,64]{3,2,1,0:T(4,128)S(1)}, f32[1,1,4,64]{3,2,1,0:T(4,128)S(1)}, u32[]{:S(2)}, u32[]{:S(2)}) collective-permute-start(f32[1,1,4,64]{3,2,1,0:T(4,128)S(1)} %maximum_bitcast_fusion), channel_id=1, source_target_pairs={{16,0},{32,16},{48,32},{64,48},{80,64},{96,80},{112,96},{128,112},... | collective-permute-start | bytes 3080 | tf_op jit(solution)/shard_map/ppermute | solution.py:33
  16.4 6.4 %collective-permute-start = (f32[1,1,4,64]{3,2,1,0:T(4,128)S(1)}, f32[1,1,4,64]{3,2,1,0:T(4,128)S(1)}, u32[]{:S(2)}, u32[]{:S(2)}) collective-permute-start(f32[1,1,4,64]{3,2,1,0:T(4,128)S(1)} %maximum_bitcast_fusion), channel_id=1, source_target_pairs={{0,16},{16,32},{32,48},{48,64},{64,80},{80,96},{96,112},{112,128},... | collective-permute-start | bytes 3080 | tf_op jit(solution)/shard_map/ppermute | solution.py:31
  19.0 13.7 %copy-start.57 = (s32[384]{0:T(512)}, s32[384]{0:T(512)S(1)}, u32[]{:S(2)}) copy-start(s32[384]{0:T(512)S(1)} %fusion.154) | copy-start | bytes 4612
  19.7 19.7 %copy-start.40 = (f32[384]{0:T(512)}, f32[384]{0:T(512)S(1)}, u32[]{:S(2)}) copy-start(f32[384]{0:T(512)S(1)} %fusion.150) | copy-start | bytes 4612
  20.7 16.8 %copy-start.50 = (s32[1024]{0:T(1024)}, s32[1024]{0:T(1024)S(1)}, u32[]{:S(2)}) copy-start(s32[1024]{0:T(1024)S(1)} %pad_clamp_fusion) | copy-start | bytes 12292
  22.8 9.3 %collective-permute-start.3 = (f32[3,1,4,64]{3,2,1,0:T(4,128)S(1)}, f32[3,1,4,64]{3,2,1,0:T(4,128)S(1)}, u32[]{:S(2)}, u32[]{:S(2)}) collective-permute-start(f32[3,1,4,64]{3,2,1,0:T(4,128)S(1)} %pad_maximum_fusion.9), channel_id=1, source_target_pairs={{1,0},{2,1},{3,2},{4,3},{5,4},{6,5},{7,6},{8,7},{9,8},{10,9},{11,1... | collective-permute-start | bytes 9224 | tf_op jit(solution)/shard_map/ppermute | solution.py:33
  26.8 5.9 %collective-permute-start.2 = (f32[3,1,4,64]{3,2,1,0:T(4,128)S(1)}, f32[3,1,4,64]{3,2,1,0:T(4,128)S(1)}, u32[]{:S(2)}, u32[]{:S(2)}) collective-permute-start(f32[3,1,4,64]{3,2,1,0:T(4,128)S(1)} %pad_maximum_fusion.9), channel_id=1, source_target_pairs={{0,1},{1,2},{2,3},{3,4},{4,5},{5,6},{6,7},{7,8},{8,9},{9,10},{10,1... | collective-permute-start | bytes 9224 | tf_op jit(solution)/shard_map/ppermute | solution.py:31
  32.0 43.3 %copy-start.82 = (f32[8]{0:T(128)}, f32[8]{0:T(128)S(1)}, u32[]{:S(2)}) copy-start(f32[8]{0:T(128)S(1)} %convert_multiply_fusion.1) | copy-start | bytes 100
  37.4 37.9 %copy-start.47 = (f32[384]{0:T(512)}, f32[384]{0:T(512)S(1)}, u32[]{:S(2)}) copy-start(f32[384]{0:T(512)S(1)} %get-tuple-element.64) | copy-start | bytes 4612
  37.4 37.9 %copy-start.61 = (f32[384]{0:T(512)}, f32[384]{0:T(512)S(1)}, u32[]{:S(2)}) copy-start(f32[384]{0:T(512)S(1)} %get-tuple-element.62) | copy-start | bytes 4612
  37.4 37.9 %copy-start.64 = (f32[384]{0:T(512)}, f32[384]{0:T(512)S(1)}, u32[]{:S(2)}) copy-start(f32[384]{0:T(512)S(1)} %get-tuple-element.63) | copy-start | bytes 4612
  47.3 27.9 %copy-start.74 = (f32[64,8]{0,1:T(8,128)S(1)}, f32[64,8]{0,1:T(8,128)}, u32[]{:S(2)}) copy-start(f32[64,8]{0,1:T(8,128)} %param.32) | copy-start | bytes 6148
  47.3 28.3 %copy-start.71 = (f32[64,64]{1,0:T(8,128)S(1)}, f32[64,64]{1,0:T(8,128)}, u32[]{:S(2)}) copy-start(f32[64,64]{1,0:T(8,128)} %param.33) | copy-start | bytes 49156
  48.1 16.4 %collective-permute-start.5 = (f32[1,1,1152,64]{2,3,1,0:T(8,128)S(1)}, f32[1,1,1152,64]{2,3,1,0:T(8,128)S(1)}, u32[]{:S(2)}, u32[]{:S(2)}) collective-permute-start(f32[1,1,1152,64]{2,3,1,0:T(8,128)S(1)} %bitcast.399), channel_id=1, source_target_pairs={{16,0},{32,16},{48,32},{64,48},{80,64},{96,80},{112,96},{128,112},... | collective-permute-start | bytes 884744 | tf_op jit(solution)/shard_map/ppermute | solution.py:33
  51.5 13.0 %collective-permute-start.4 = (f32[1,1,1152,64]{2,3,1,0:T(8,128)S(1)}, f32[1,1,1152,64]{2,3,1,0:T(8,128)S(1)}, u32[]{:S(2)}, u32[]{:S(2)}) collective-permute-start(f32[1,1,1152,64]{2,3,1,0:T(8,128)S(1)} %bitcast.400), channel_id=1, source_target_pairs={{0,16},{16,32},{32,48},{48,64},{64,80},{80,96},{96,112},{112,128},... | collective-permute-start | bytes 884744 | tf_op jit(solution)/shard_map/ppermute | solution.py:31
  64.6 18.0 %collective-permute-start.7 = (f32[3,1,1152,64]{2,3,1,0:T(8,128)S(1)}, f32[3,1,1152,64]{2,3,1,0:T(8,128)S(1)}, u32[]{:S(2)}, u32[]{:S(2)}) collective-permute-start(f32[3,1,1152,64]{2,3,1,0:T(8,128)S(1)} %pad_maximum_fusion.4), channel_id=1, source_target_pairs={{1,0},{2,1},{3,2},{4,3},{5,4},{6,5},{7,6},{8,7},{9,8},{10,9},{11,1... | collective-permute-start | bytes 2654216 | tf_op jit(solution)/shard_map/ppermute | solution.py:33
  66.7 17.1 %collective-permute-start.6 = (f32[3,1,1152,64]{2,3,1,0:T(8,128)S(1)}, f32[3,1,1152,64]{2,3,1,0:T(8,128)}, u32[]{:S(2)}, u32[]{:S(2)}) collective-permute-start(f32[3,1,1152,64]{2,3,1,0:T(8,128)S(1)} %pad_maximum_fusion.4), channel_id=1, source_target_pairs={{0,1},{1,2},{2,3},{3,4},{4,5},{5,6},{6,7},{7,8},{8,9},{9,10},{10,1... | collective-permute-start | bytes 2654216 | tf_op jit(solution)/shard_map/ppermute | solution.py:31
  121.1 42.5 %collective-permute-start.8 = (f32[1155,3,64]{0,2,1:T(8,128)}, f32[1155,3,64]{0,2,1:T(8,128)}, u32[]{:S(2)}, u32[]{:S(2)}) collective-permute-start(f32[1155,3,64]{0,2,1:T(8,128)} %get-tuple-element.30), channel_id=1, source_target_pairs={{0,16},{16,32},{32,48},{48,64},{64,80},{80,96},{96,112},{112,128},... | collective-permute-start | bytes 2661128 | tf_op jit(solution)/shard_map/ppermute | solution.py:21
  123.1 44.7 %collective-permute-start.9 = (f32[1155,3,64]{0,2,1:T(8,128)}, f32[1155,3,64]{0,2,1:T(8,128)}, u32[]{:S(2)}, u32[]{:S(2)}) collective-permute-start(f32[1155,3,64]{0,2,1:T(8,128)} %get-tuple-element.31), channel_id=1, source_target_pairs={{0,496},{16,0},{32,16},{48,32},{64,48},{80,64},{96,80},{112,96},{1... | collective-permute-start | bytes 2661128 | tf_op jit(solution)/shard_map/ppermute | solution.py:21
  132.1 43.4 %copy-start.30 = (f32[128,128]{1,0:T(8,128)S(1)}, f32[128,128]{1,0:T(8,128)}, u32[]{:S(2)}) copy-start(f32[128,128]{1,0:T(8,128)} %copy-done.29) | copy-start | bytes 196612
  169.7 7.8 %collective-permute-start.10 = (f32[1155,64]{0,1:T(8,128)S(1)}, f32[1155,64]{0,1:T(8,128)S(1)}, u32[]{:S(2)}, u32[]{:S(2)}) collective-permute-start(f32[1155,64]{0,1:T(8,128)S(1)} %get-tuple-element.34), channel_id=1, source_target_pairs={{0,1},{1,2},{2,3},{3,4},{4,5},{5,6},{6,7},{7,8},{8,9},{9,10},{10,1... | collective-permute-start | bytes 887048 | tf_op jit(solution)/shard_map/ppermute | solution.py:21
  173.6 12.0 %collective-permute-start.11 = (f32[1155,64]{0,1:T(8,128)S(1)}, f32[1155,64]{0,1:T(8,128)S(1)}, u32[]{:S(2)}, u32[]{:S(2)}) collective-permute-start(f32[1155,64]{0,1:T(8,128)S(1)} %get-tuple-element.35), channel_id=1, source_target_pairs={{0,15},{1,0},{2,1},{3,2},{4,3},{5,4},{6,5},{7,6},{8,7},{9,8},{10,9... | collective-permute-start | bytes 887048 | tf_op jit(solution)/shard_map/ppermute | solution.py:21
  176.4 18.2 %copy-start.26 = (f32[3,128,128]{2,1,0:T(8,128)S(1)}, f32[3,128,128]{2,1,0:T(8,128)}, u32[]{:S(2)}) copy-start(f32[3,128,128]{2,1,0:T(8,128)} %param.29) | copy-start | bytes 589828
  207.5 8.3 %collective-permute-start.12 = (f32[3,3,64]{0,2,1:T(8,128)S(1)}, f32[3,3,64]{0,2,1:T(8,128)S(1)}, u32[]{:S(2)}, u32[]{:S(2)}) collective-permute-start(f32[3,3,64]{0,2,1:T(8,128)S(1)} %get-tuple-element.44), channel_id=1, source_target_pairs={{0,16},{16,32},{32,48},{48,64},{64,80},{80,96},{96,112},{112,128},... | collective-permute-start | bytes 6920 | tf_op jit(solution)/shard_map/ppermute | solution.py:21
  209.4 7.1 %collective-permute-start.13 = (f32[3,3,64]{0,2,1:T(8,128)S(1)}, f32[3,3,64]{0,2,1:T(8,128)S(1)}, u32[]{:S(2)}, u32[]{:S(2)}) collective-permute-start(f32[3,3,64]{0,2,1:T(8,128)S(1)} %get-tuple-element.45), channel_id=1, source_target_pairs={{0,496},{16,0},{32,16},{48,32},{64,48},{80,64},{96,80},{112,96},{1... | collective-permute-start | bytes 6920 | tf_op jit(solution)/shard_map/ppermute | solution.py:21
  216.5 5.0 %collective-permute-start.14 = (f32[3,64]{0,1:T(8,128)S(1)}, f32[3,64]{0,1:T(8,128)S(1)}, u32[]{:S(2)}, u32[]{:S(2)}) collective-permute-start(f32[3,64]{0,1:T(8,128)S(1)} %get-tuple-element.49), channel_id=1, source_target_pairs={{0,1},{1,2},{2,3},{3,4},{4,5},{5,6},{6,7},{7,8},{8,9},{9,10},{10,1... | collective-permute-start | bytes 2312 | tf_op jit(solution)/shard_map/ppermute | solution.py:21
  219.4 8.8 %collective-permute-start.15 = (f32[3,64]{0,1:T(8,128)S(1)}, f32[3,64]{0,1:T(8,128)S(1)}, u32[]{:S(2)}, u32[]{:S(2)}) collective-permute-start(f32[3,64]{0,1:T(8,128)S(1)} %get-tuple-element.50), channel_id=1, source_target_pairs={{0,15},{1,0},{2,1},{3,2},{4,3},{5,4},{6,5},{7,6},{8,7},{9,8},{10,9... | collective-permute-start | bytes 2312 | tf_op jit(solution)/shard_map/ppermute | solution.py:21
  (70 other events, 242.2 us)
where the time goes:
time: 231 us; the launch traced here: 230 us
  waiting for transfers between devices  70.9 us (31%)
  starting transfers between devices  63.2 us (27%)
  local copies, waits for them, and re-layouts  33.7 us (15%)
  other arithmetic  32.6 us (14%)
  matrix products  27 us (12%)
  between operations  2.66 us (1%)
    ppermute x8, waiting for transfers between devices, from_behind(): return lax.ppermute(value, axis, pairs)  50.7 us
    ppermute x8, starting transfers between devices, from_behind(): return lax.ppermute(value, axis, pairs)  25.3 us
    ppermute x4, starting transfers between devices, extended(): lax.ppermute(head, axis, [((i + 1) % count, i) for i in range(count)])  21.5 us
    dot_general x24, matrix products, product(): jnp.dot(left_side, right_side, precision=precise, preferred_element_type=...  16.9 us
    ppermute x4, starting transfers between devices, extended(): lax.ppermute(tail, axis, [(i, (i + 1) % count) for i in range(count)])  16.3 us
    ppermute x4, waiting for transfers between devices, extended(): lax.ppermute(head, axis, [((i + 1) % count, i) for i in range(count)])  16.3 us
    unnamed x174, local copies, waits for them, and re-layouts  9.83 us
    scatter-add x1, other arithmetic, layer_two(): jnp.concatenate([features, ghost_features], axis=1)[:, table_index]  5.87 us
  transfers between devices with their start and end apart: 16, of which 11 were waited for; matrix products, arithmetic and copies ran while one was open for 6% of the time, Pallas kernels for 0%

commit v1 on v0

v1 whole, which is shorter than its diff:
```python
import math

import jax
import jax.numpy as jnp
import numpy as np
from jax import lax
from jax.experimental import pallas as pl
from jax.experimental.pallas import tpu as pltpu
from jax.sharding import PartitionSpec as P

SIDE = 8
SPACING = 1.75
CUTOFF = 5.0
SOFTEN = 0.25
STRENGTH = 2.0
F32 = jnp.float32
BF16 = jnp.bfloat16
INTERPRET = False

TILES = 11
EDGES = TILES * 128
EDGES_TWO = 7 * 128
EDGES_BACK = 6 * 128


def tables():
    lane = np.arange(128)
    site_x, site_y = lane // 16, lane // 2 % 8

    def outer(site):
        low = site >= 4
        return np.where(low, -1, 1), np.where(low, 8 - site, site + 1)

    block_x, ring_x = outer(site_x)
    block_y, ring_y = outer(site_y)
    none = np.zeros(128, np.int64)
    rings = np.concatenate([ring_x, ring_y, np.maximum(ring_x, ring_y)])
    blocks_x = np.concatenate([block_x, none, block_x])
    blocks_y = np.concatenate([none, block_y, block_y])
    source = np.concatenate([none, none + 1, none + 2])
    order = np.argsort(rings, kind="stable")
    atoms = np.zeros((8, 512), np.int64)
    atoms[0] = np.concatenate([lane, np.tile(lane, 3)[order]])
    atoms[1] = np.concatenate([none, source[order]])
    atoms[2] = np.concatenate([none, blocks_x[order]])
    atoms[3] = np.concatenate([none, blocks_y[order]])
    code = 3 * (atoms[2] + 1) + atoms[3] + 1
    atoms[4] = code
    atoms[5] = code * 192 + atoms[0]
    edges = np.zeros((8, EDGES), np.int64)
    tile_code = code.reshape(4, 128)
    edges[0] = np.concatenate(
        [tile_code[0]] * 3
        + [tile_code[1]] * 3
        + [tile_code[2][lane % 32]]
        + [tile_code[2]] * 3
        + [tile_code[3][lane % 8]]
    )
    two = np.where(lane < 96, lane // 32, 9)
    three = np.where(lane < 24, lane // 8, 9)
    slots = [none, none + 1, none + 2]
    edges[1] = np.concatenate(slots + slots + [two] + slots + [three])
    near = (lane < 72).astype(np.int64)
    edges[2] = np.concatenate([none + 1] * 3 + [near] * 3 + [none] * 5)
    return atoms.astype(np.int32), edges.astype(np.int32)


ATOM_TABLE, EDGE_TABLE = tables()


def rounded(x):
    return x.astype(BF16).astype(F32)


def split(x):
    high = x.astype(BF16)
    return high, (x - high.astype(F32)).astype(BF16)


def mm(a, b):
    return lax.dot_general(a, b, (((1,), (0,)), ((), ())), preferred_element_type=F32)


def mm_nt(a, b):
    return lax.dot_general(a, b, (((1,), (1,)), ((), ())), preferred_element_type=F32)


def dots(a, b):
    return mm(a[0], b[0]) + mm(a[0], b[1]) + mm(a[1], b[0])


def dot3(a, b):
    return dots(split(a), split(b))


def silu_pair(x):
    gate = 1.0 / (1.0 + jnp.exp(-x))
    return x * gate, gate * (1.0 + x * (1.0 - gate))


def lanes_from(x, index):
    return jnp.take_along_axis(x, index, axis=1, mode="promise_in_bounds")


def column_of(row, width=128):
    return jnp.broadcast_to(row, (width, row.shape[1])).T


def roll_up(x, amount):
    return pltpu.roll(x, 128 - amount, 1)


def pack_kernel(*refs):
    sources, out, copies, sems = refs[:6], refs[6], refs[7:13], refs[13]
    moves = [pltpu.make_async_copy(s, d, sems.at[i]) for i, (s, d) in enumerate(zip(sources, copies))]
    for move in moves:
        move.start()
    for move in moves:
        move.wait()
    pos, species, senders, counts, owners, send_list = copies
    for i in range(3):
        out[i : i + 1, :] = pos[i]
        out[4 + i : 5 + i, :] = senders[i].astype(F32)
        out[8 + i : 9 + i, :] = owners[i].astype(F32)
    out[3:4, :] = species[...].astype(F32)
    out[7:8, :] = counts[...].astype(F32)
    picked = jnp.broadcast_to(send_list[...].astype(F32), (128, 64)).T
    lane = lax.broadcasted_iota(jnp.int32, (64, 128), 1).astype(F32)
    row = lax.broadcasted_iota(jnp.int32, (64, 128), 0).astype(F32)
    slot = jnp.max(jnp.where(picked == lane, row, -1.0), axis=0, keepdims=True)
    out[11:16, :] = jnp.broadcast_to(slot, (5, 128))


def main_kernel(
    odd,
    mid,
    near_a,
    near_b,
    atom_table_hbm,
    edge_table_hbm,
    embedding_hbm,
    in_one_hbm,
    mid_one_hbm,
    out_one_hbm,
    mixing_hbm,
    square_mix_hbm,
    readout_one_hbm,
    in_two_hbm,
    mid_two_hbm,
    out_two_hbm,
    mix_two_hbm,
    read_hidden_hbm,
    read_out_hbm,
    forces,
    energies,
    hot0,
    hot1,
    hot2,
    emb_tab,
    spec_row,
    emb_edge,
    carried,
    shape_row,
    moments,
    squares,
    scalar_feat,
    feats,
    gathered_ref,
    proj,
    mix_split,
    mix_back,
    w_two,
    queue,
    square_grad,
    shape_grad,
    radial_grad,
    atom_table,
    edge_table,
    embedding,
    in_one,
    mid_one,
    out_one,
    mixing,
    square_mix,
    readout_one,
    in_two,
    mid_two,
    out_two,
    mix_two,
    read_hidden,
    read_out,
    sems,
):
    moves = [
        pltpu.make_async_copy(source, target, sems.at[i])
        for i, (source, target) in enumerate(
            (
                (atom_table_hbm, atom_table),
                (edge_table_hbm, edge_table),
                (embedding_hbm, embedding),
                (in_one_hbm, in_one),
                (mid_one_hbm, mid_one),
                (out_one_hbm, out_one),
                (mixing_hbm, mixing),
                (square_mix_hbm, square_mix),
                (readout_one_hbm, readout_one),
                (in_two_hbm, in_two),
                (mid_two_hbm, mid_two),
                (out_two_hbm, out_two),
                (mix_two_hbm, mix_two),
                (read_hidden_hbm, read_hidden),
                (read_out_hbm, read_out),
            )
        )
    ]
    for move in moves:
        move.start()
    moves[0].wait()
    moves[1].wait()
    lane256 = lax.broadcasted_iota(jnp.int32, (16, 256), 1) % 128
    from_a = (lane256 // 64) == odd[0]
    x_outer = jnp.where(from_a, near_a[...], near_b[...])
    own = mid[:, 0:128]
    sources = (x_outer[:, 0:128], mid[:, 128:256], x_outer[:, 128:256])
    row16 = lax.broadcasted_iota(jnp.int32, (16, 128), 0)
    atom_tiles = [own]
    key_b = []
    for t in range(4):
        cut = slice(128 * t, 128 * t + 128)
        if t:
            index = jnp.broadcast_to(atom_table[0:1, cut], (16, 128))
            which = jnp.broadcast_to(atom_table[1:2, cut], (16, 128))
            picked = [lanes_from(s, index) for s in sources]
            tile = jnp.where(which == 0, picked[0], jnp.where(which == 1, picked[1], picked[2]))
            block_x = jnp.broadcast_to(atom_table[2:3, cut].astype(F32), (16, 128))
            block_y = jnp.broadcast_to(atom_table[3:4, cut].astype(F32), (16, 128))
            shift = jnp.where(row16 == 0, block_x, jnp.where(row16 == 1, block_y, 0.0))
            atom_tiles.append(tile + shift * (SPACING * SIDE))
        slot = atom_tiles[t][11:12, :]
        code = atom_table[4:5, cut].astype(F32)
        key_b.append(jnp.where(slot < 0.0, -1.0, code * 192.0 + 128.0 + slot))
    lane16 = lax.broadcasted_iota(jnp.int32, (16, 128), 1)
    pack_two = lanes_from(atom_tiles[2], lane16 % 32)
    pack_three = lanes_from(atom_tiles[3], lane16 % 8)
    t0, t1, t2, t3 = atom_tiles
    receivers = jnp.concatenate([t0] * 3 + [t1] * 3 + [pack_two] + [t2] * 3 + [pack_three], 1)

    slot_row = edge_table[1:2, :]
    sent = jnp.where(
        slot_row == 0,
        receivers[4:5],
        jnp.where(slot_row == 1, receivers[5:6], receivers[6:7]),
    ).astype(jnp.int32)
    owned = jnp.where(
        slot_row == 0,
        receivers[8:9],
        jnp.where(slot_row == 1, receivers[9:10], receivers[10:11]),
    )
    live = (slot_row < receivers[7:8].astype(jnp.int32)).astype(F32)
    ghost = sent - 128
    block = lax.shift_right_arithmetic(ghost, 6)
    block = block + (block >= 4).astype(jnp.int32)
    code_row = edge_table[0:1, :]
    key = jnp.where(
        sent < 128,
        code_row * 192 + sent,
        (code_row + block - 4) * 192 + 128 + (ghost & 63),
    ).astype(F32)
    for c in range(4):
        cut = slice(128 * c, 128 * c + 128)
        plain = column_of(atom_table[5:6, cut].astype(F32))
        listed = column_of(key_b[c])
        for e in range(TILES):
            if e < 3 and c > 1:
                continue
            wanted = key[:, 128 * e : 128 * e + 128]
            hit = jnp.where((plain == wanted) | (listed == wanted), 1.0, 0.0).astype(BF16)
            if e < 3:
                hot0[cut, 128 * e : 128 * e + 128] = hit
            elif e < 7:
                hot1[cut, 128 * (e - 3) : 128 * (e - 3) + 128] = hit
            else:
                hot2[cut, 128 * (e - 7) : 128 * (e - 7) + 128] = hit

    raw = jnp.concatenate([t[0:8] for t in atom_tiles], 1)
    first = rounded(raw)
    second = rounded(raw - first)
    third = rounded(raw - first - second)
    terms = jnp.concatenate([first, second, third, third], 0).astype(BF16)
    found = jnp.concatenate(
        [mm(terms[:, 0:256], hot0[...]), mm(terms, hot1[...]), mm(terms, hot2[...])], 1
    )
    found = found[0:8] + found[8:16] + found[16:24]
    away = [found[i : i + 1] - receivers[i : i + 1] for i in range(3)]
    spec_row[0:1, :] = found[3:4]
    spec_row[1:2, :] = live

    radius_sq = away[0] * away[0] + away[1] * away[1] + away[2] * away[2] + SOFTEN
    radius = jnp.sqrt(radius_sq)
    inverse = 1.0 / radius
    ux, uy, uz = [a * inverse for a in away]
    scaled = jnp.minimum(radius / CUTOFF, 1.0)
    s2 = scaled * scaled
    s3 = s2 * scaled
    s6 = s3 * s3
    envelope = 1.0 - 28.0 * s6 + 48.0 * s6 * scaled - 21.0 * s6 * s2
    slope = jnp.where(radius < CUTOFF, 1.0 / CUTOFF, 0.0)
    gap = 1.0 - scaled
    envelope_slope = -168.0 * s3 * s2 * gap * gap * slope
    order = (lax.broadcasted_iota(jnp.int32, (8, EDGES), 0) + 1).astype(F32)
    phase = order * (math.pi * scaled)
    factor = math.sqrt(2.0 / CUTOFF)
    sines = factor * jnp.sin(phase)
    basis = sines * (envelope * inverse)
    near = slice(0, EDGES_BACK)
    cosines = factor * jnp.cos(phase[:, near])
    basis_slope = (
        order[:, near] * cosines * (math.pi * slope * envelope * inverse)[:, near]
        + sines[:, near] * ((envelope_slope - envelope * inverse) * inverse)[:, near]
    )
    r3, r5, r15 = math.sqrt(3.0), math.sqrt(5.0), math.sqrt(15.0)
    shape_row[0:9, :] = jnp.concatenate(
        [
            jnp.ones_like(ux),
            r3 * ux,
            r3 * uy,
            r3 * uz,
            r15 * ux * uy,
            r15 * uy * uz,
            (0.5 * r5) * (2.0 * uz * uz - ux * ux - uy * uy),
            r15 * ux * uz,
            (0.5 * r15) * (ux * ux - uy * uy),
        ],
        0,
    )
    pair = owned * live * STRENGTH * jnp.exp(-radius)
    pair_slope = (pair * (envelope_slope - envelope))[:, near]
    pair = pair * envelope
    pair_own = pair[:, 0:128] + pair[:, 128:256] + pair[:, 256:384]

    for move in moves[2:]:
        move.wait()
    for z in range(5):
        emb_tab[z] = column_of(embedding[z : z + 1, :])

    def element(code):
        value = emb_tab[0]
        for z in range(1, 5):
            value = jnp.where(code == float(z), emb_tab[z], value)
        return value

    def embed_edges(e, carry):
        at = pl.ds(pl.multiple_of(e * 128, 128), 128)
        emb_edge[:, at] = element(spec_row[0:1, at]) * spec_row[1:2, at]
        return carry

    lax.fori_loop(0, TILES, embed_edges, 0)

    basis_s = split(basis)
    pre1 = dots(split(in_one[...].T), basis_s)
    hid1, dhid1 = silu_pair(pre1)
    pre1 = dots(split(mid_one[...]), split(hid1))
    top1, dtop1 = silu_pair(pre1)
    dhid1, dtop1 = dhid1[:, near], dtop1[:, near]
    top1 = split(top1)
    for g in range(3):
        weight = dots(split(out_one[:, 128 * g : 128 * g + 128].T), top1)
        carried[g] = weight * emb_edge[...]
    basis_two = (basis_s[0][:, 0:EDGES_TWO], basis_s[1][:, 0:EDGES_TWO])
    pre2 = dots(split(in_two[...].T), basis_two)
    hid2, dhid2 = silu_pair(pre2)
    pre2 = dots(split(mid_two[...]), split(hid2))
    top2, dtop2 = silu_pair(pre2)
    dhid2, dtop2 = dhid2[:, near], dtop2[:, near]
    top2 = split(top2)
    for g in range(3):
        w_two[g] = dots(split(out_two[:, 128 * g : 128 * g + 128].T), top2)

    for g in range(3):
        high, low = split(mixing[g])
        mix_split[g, 0:128, :] = high
        mix_split[g, 128:256, :] = low
        high, low = split(mixing[g].T)
        mix_back[g, 0:128, :] = high
        mix_back[g, 128:256, :] = low

    def degree(m):
        return (m > 0).astype(jnp.int32) + (m > 3).astype(jnp.int32)

    def moment(m, g):
        y = shape_row[pl.ds(m, 1), :]

        def part(e):
            at = slice(128 * e, 128 * e + 128)
            return carried[g, :, at] * y[:, at]

        tail = part(10)
        value = jnp.concatenate(
            [
                part(0) + part(1) + part(2),
                part(3) + part(4) + part(5),
                part(7) + part(8) + part(9),
                tail + roll_up(tail, 8) + roll_up(tail, 16),
            ],
            1,
        ) * (1.0 / 3.0)
        moments[m] = value
        high, low = split(value)
        both = mm(mix_split[g], high)
        mixed = both[0:128] + both[128:256] + mm(mix_split[g, 0:128, :], low)
        return value, mixed

    value, mixed = moment(0, 0)
    squares[...] = value * value
    scalar_feat[...] = mixed

    def moment_step(m, carry):
        value, mixed = moment(m, degree(m))
        squares[...] += value * value
        high, low = split(mixed)
        feats[m, 0:128, :] = high
        feats[m, 128:256, :] = low
        return carry

    lax.fori_loop(1, 9, moment_step, 0)
    element_rows = jnp.concatenate([t[3:4] for t in atom_tiles], 1)
    scalar = scalar_feat[...] + dot3(square_mix[...], squares[...])
    scalar = scalar + jnp.concatenate(
        [element(element_rows[:, 128 * t : 128 * t + 128]) for t in range(4)], 1
    )
    scalar_feat[...] = scalar
    high, low = split(scalar)
    feats[0, 0:128, :] = high
    feats[0, 128:256, :] = low

    proj[...] = jnp.zeros_like(proj)

    def gather_step(m, carry):
        g = degree(m)
        left = feats[m]
        part = mm(left[:, 0:256], hot0[...])
        rest = mm(left, hot1[...])
        part = part[0:128] + part[128:256]
        rest = rest[0:128] + rest[128:256]
        gathered_ref[m, :, 0:384] = part
        gathered_ref[m, :, 384:896] = rest
        y = shape_row[pl.ds(m, 1), :]
        proj[g, :, 0:384] += part * y[:, 0:384]
        proj[g, :, 384:896] += rest * y[:, 384:896]
        return carry

    lax.fori_loop(0, 9, gather_step, 0)
    live_two = live[:, 0:EDGES_TWO]
    term = (w_two[0] * proj[0] + w_two[1] * proj[1] + w_two[2] * proj[2]) * live_two
    tail = term[:, 768:896]
    total = jnp.concatenate(
        [
            term[:, 0:128] + term[:, 128:256] + term[:, 256:384],
            term[:, 384:512] + term[:, 512:640] + term[:, 640:768],
            tail + roll_up(tail, 32) + roll_up(tail, 64),
        ],
        1,
    ) * (1.0 / 3.0)
    refined = dot3(mix_two[...], total) + scalar_feat[:, 0:384]
    hidden = dot3(read_hidden[...], refined)
    act, dact = silu_pair(hidden)
    out_column = jnp.broadcast_to(column_of(read_out[...])[:, 0:1], (16, 384))
    one_column = column_of(readout_one[...])
    energies[...] = (
        jnp.sum(act[:, 0:128] * out_column[:, 0:128], axis=0, keepdims=True)
        + jnp.sum(scalar_feat[:, 0:128] * one_column, axis=0, keepdims=True)
        + pair_own
    )

    refined_grad = dot3(read_hidden[...].T, dact * out_column)
    total_grad = dot3(mix_two[...].T, refined_grad) * (1.0 / 3.0)
    lane128 = lax.broadcasted_iota(jnp.int32, (128, 128), 1)
    tail = jnp.where(lane128 < 32, total_grad[:, 256:384], 0.0)
    tail = tail + pltpu.roll(tail, 32, 1) + pltpu.roll(tail, 64, 1)
    grad0, grad1 = total_grad[:, 0:128], total_grad[:, 128:256]
    term_grad = jnp.concatenate([grad0] * 3 + [grad1] * 3 + [tail], 1) * live_two
    for g in range(3):
        queue[g] = term_grad * w_two[g]
        proj[g, :, near] = term_grad[:, near] * proj[g, :, near]
    radial_grad[...] = jnp.zeros_like(radial_grad)

    def back(m, g, first):
        y = shape_row[pl.ds(m, 1), :]
        q = queue[g]
        high, low = split(q * y[:, 0:EDGES_TWO])
        left = jnp.concatenate([high, low], 0)
        grad = mm_nt(left[:, 0:384], hot0[...]) + mm_nt(left[:, 384:896], hot1[0:256, :])
        grad = grad[0:128] + grad[128:256]
        if first:
            grad = grad + refined_grad[:, 0:256] + jnp.concatenate([one_column] * 2, 1)
            square_grad[...] = 2.0 * dot3(square_mix[...].T, grad)
        high, low = split(grad)
        both = mm(mix_back[g], high)
        grad = both[0:128] + both[128:256] + mm(mix_back[g, 0:128, :], low)
        grad = (grad + square_grad[...] * moments[m, :, 0:256]) * (1.0 / 3.0)
        wide = jnp.concatenate([grad[:, 0:128]] * 3 + [grad[:, 128:256]] * 3, 1)
        both = q[:, near] * gathered_ref[m, :, near] + wide * carried[g, :, near]
        shape_grad[pl.ds(m, 1), :] = jnp.sum(both, axis=0, keepdims=True)
        radial_grad[g] += wide * y[:, near]

    back(0, 0, True)

    def back_step(m, carry):
        back(m, degree(m), False)
        return carry

    lax.fori_loop(1, 9, back_step, 0)

    def radial_back(grads, weight_out, weight_mid, weight_in, dtop, dhid):
        top_grad = 0.0
        for g in range(3):
            top_grad = top_grad + dot3(weight_out[:, 128 * g : 128 * g + 128], grads[g])
        hid_grad = dot3(weight_mid[...].T, top_grad * dtop)
        return dot3(weight_in[...], hid_grad * dhid)

    ones = [radial_grad[g] * emb_edge[:, near] for g in range(3)]
    basis_grad = radial_back(ones, out_one, mid_one, in_one, dtop1, dhid1)
    twos = [proj[g, :, near] for g in range(3)]
    basis_grad = basis_grad + radial_back(twos, out_two, mid_two, in_two, dtop2, dhid2)

    ux, uy, uz, inverse = ux[:, near], uy[:, near], uz[:, near], inverse[:, near]
    ym = [shape_grad[m : m + 1, :] for m in range(9)]
    gx = r3 * ym[1] + r15 * (uy * ym[4] + uz * ym[7] + ux * ym[8]) - r5 * ux * ym[6]
    gy = r3 * ym[2] + r15 * (ux * ym[4] + uz * ym[5] - uy * ym[8]) - r5 * uy * ym[6]
    gz = r3 * ym[3] + r15 * (uy * ym[5] + ux * ym[7]) + 2.0 * r5 * uz * ym[6]
    along = jnp.sum(basis_grad * basis_slope, axis=0, keepdims=True) + pair_slope
    along = along - (gx * ux + gy * uy + gz * uz) * inverse
    keep = edge_table[2:3, near].astype(F32)
    edge_grad = jnp.concatenate(
        [(gx * inverse + along * ux) * keep, (gy * inverse + along * uy) * keep,
         (gz * inverse + along * uz) * keep, jnp.zeros((5, EDGES_BACK), F32)],
        0,
    )
    high = rounded(edge_grad)
    left = jnp.concatenate([high, edge_grad - high], 0).astype(BF16)
    pulled = mm_nt(left[:, 0:384], hot0[0:128, :]) + mm_nt(left[:, 384:768], hot1[0:128, 0:384])
    pulled = pulled[0:8] + pulled[8:16]
    mine = edge_grad[:, 0:128] + edge_grad[:, 128:256] + edge_grad[:, 256:384]
    total = mine - pulled
    for i in range(3):
        forces[i] = total[i : i + 1]


def swap(value, axis, odd):
    count = lax.axis_size(axis)
    pairs = [(i, (((i - odd) ^ 1) + odd) % count) for i in range(count)]
    return lax.ppermute(value, axis, pairs)


def local(
    positions,
    species,
    senders,
    counts,
    owners,
    send_list,
    embedding,
    radial_in_one,
    radial_mid_one,
    radial_out_one,
    mixing,
    square_mix,
    readout_one,
    radial_in_two,
    radial_mid_two,
    radial_out_two,
    mix_two,
    read_hidden,
    read_out,
):
    packed = pl.pallas_call(
        pack_kernel,
        out_shape=jax.ShapeDtypeStruct((16, 128), F32),
        in_specs=[pl.BlockSpec(memory_space=pltpu.HBM)] * 6,
        out_specs=pl.BlockSpec(memory_space=pltpu.VMEM),
        scratch_shapes=[
            pltpu.VMEM((3, 1, 128), F32),
            pltpu.VMEM((1, 128), jnp.int32),
            pltpu.VMEM((3, 1, 128), jnp.int32),
            pltpu.VMEM((1, 128), jnp.int32),
            pltpu.VMEM((3, 1, 128), jnp.int32),
            pltpu.VMEM((1, 64), jnp.int32),
            pltpu.SemaphoreType.DMA((6,)),
        ],
        interpret=INTERPRET,
    )(
        positions.reshape(3, 1, 128),
        species[0],
        senders.reshape(3, 1, 128),
        counts[0],
        owners.reshape(3, 1, 128),
        send_list[0],
    )
    near_a, near_b = swap(packed, "gy", 0), swap(packed, "gy", 1)
    odd_y = lax.axis_index("gy") % 2
    lane = lax.broadcasted_iota(jnp.int32, (16, 128), 1)
    outer = jnp.where(lane // 8 % 2 == odd_y, near_a, near_b)
    mid = jnp.concatenate([packed, outer], 1)
    near_a, near_b = swap(mid, "gx", 0), swap(mid, "gx", 1)
    odd_x = (lax.axis_index("gx") % 2).astype(jnp.int32).reshape(1)
    held = (
        jnp.asarray(ATOM_TABLE),
        jnp.asarray(EDGE_TABLE),
        embedding.T,
        radial_in_one.T,
        radial_mid_one,
        radial_out_one.T,
        mixing,
        square_mix,
        readout_one.reshape(1, -1),
        radial_in_two.T,
        radial_mid_two,
        radial_out_two.T,
        mix_two,
        read_hidden,
        read_out.reshape(1, -1),
    )
    vmem = pl.BlockSpec(memory_space=pltpu.VMEM)
    forces, energies = pl.pallas_call(
        main_kernel,
        out_shape=(
            jax.ShapeDtypeStruct((3, 1, 128), F32),
            jax.ShapeDtypeStruct((1, 128), F32),
        ),
        in_specs=[pl.BlockSpec(memory_space=pltpu.SMEM)]
        + [vmem] * 3
        + [pl.BlockSpec(memory_space=pltpu.HBM)] * len(held),
        out_specs=(vmem, vmem),
        scratch_shapes=[
            pltpu.VMEM((256, 384), BF16),
            pltpu.VMEM((512, 512), BF16),
            pltpu.VMEM((512, 512), BF16),
            pltpu.VMEM((5, 128, 128), F32),
            pltpu.VMEM((8, EDGES), F32),
            pltpu.VMEM((128, EDGES), F32),
            pltpu.VMEM((3, 128, EDGES), F32),
            pltpu.VMEM((16, EDGES), F32),
            pltpu.VMEM((9, 128, 512), F32),
            pltpu.VMEM((128, 512), F32),
            pltpu.VMEM((128, 512), F32),
            pltpu.VMEM((9, 256, 512), BF16),
            pltpu.VMEM((9, 128, EDGES_TWO), F32),
            pltpu.VMEM((3, 128, EDGES_TWO), F32),
            pltpu.VMEM((3, 256, 128), BF16),
            pltpu.VMEM((3, 256, 128), BF16),
            pltpu.VMEM((3, 128, EDGES_TWO), F32),
            pltpu.VMEM((3, 128, EDGES_TWO), F32),
            pltpu.VMEM((128, 256), F32),
            pltpu.VMEM((16, EDGES_BACK), F32),
            pltpu.VMEM((3, 128, EDGES_BACK), F32),
        ]
        + [pltpu.VMEM(h.shape, h.dtype) for h in held]
        + [pltpu.SemaphoreType.DMA((len(held),))],
        interpret=INTERPRET,
    )(odd_x, mid, near_a, near_b, *held)
    return forces.reshape(1, 1, 3, 128), energies[None]


def solution(mesh):
    split_four = P("gx", "gy", None, None)
    split_three = P("gx", "gy", None)
    placed = (split_four, split_three, split_four, split_three, split_four, split_three)
    return jax.shard_map(
        local,
        mesh=mesh,
        in_specs=placed + (P(),) * 13,
        out_specs=(split_four, split_three),
        check_vma=False,
    )
```

time: 231 us -> 53.2 us (0.23)
  the two profiles are of different devices: /device:TPU:25 before, /device:TPU:1 now
where the time goes in v1:
time: 53.2 us; the launch traced here: 52.7 us
  Pallas kernels  23.9 us (45%)
  starting transfers between devices  23.3 us (44%)
  waiting for transfers between devices  3.5 us (7%)
  local copies, waits for them, and re-layouts  1.29 us (2%)
  between operations  0.73 us (1%)
    ppermute x4, starting transfers between devices, swap(): return lax.ppermute(value, axis, pairs)  23.3 us
    pallas_call x1, Pallas kernels, local(): pl.pallas_call(main_kernel, out_shape=(jax.ShapeDtypeStruct((3, 1, 128),...  22.4 us
    ppermute x4, waiting for transfers between devices, swap(): return lax.ppermute(value, axis, pairs)  3.5 us
    pallas_call x1, Pallas kernels, local(): pl.pallas_call(pack_kernel, out_shape=jax.ShapeDtypeStruct((16, 128), F32...  1.49 us
    unnamed x8, local copies, waits for them, and re-layouts  1.29 us
  transfers between devices with their start and end apart: 4, of which 2 were waited for; matrix products, arithmetic and copies ran while one was open for 0% of the time, Pallas kernels for 0%

profile of v1, /device:TPU:1, one launch (start us, length us, event | category | flops | bytes accessed | tf_op | source)
XLA Modules:
  0.0 52.7 jit_solution(10565816302356851745)
XLA Ops:
  0.6 1.5 %shard_map.212 = f32[16,128]{1,0:T(8,128)} custom-call(f32[3,1,128]{2,1,0:T(1,128)} %bitcast.23, s32[1,128]{1,0:T(1,128)} %bitcast.28, s32[3,1,128]{2,1,0:T(1,128)} %bitcast.24, s32[1,128]{1,0:T(1,128)} %bitcast.29, s32[3,1,128]{2,1,0:T(1,128)} %bitcast.25, s32[1,64]{1,0:T(1,128)} %bitcast.30), custom_call_target="tpu_custom_call" | custom-call | tf_op jit(solution)/shard_map/pallas_call | solution.py:576
  2.1 4.6 %collective-permute-start.1 = (f32[16,128]{1,0:T(8,128)}, f32[16,128]{1,0:T(8,128)S(1)}, u32[]{:S(2)}, u32[]{:S(2)}) collective-permute-start(f32[16,128]{1,0:T(8,128)} %shard_map.212), channel_id=1, source_target_pairs={{0,15},{1,2},{2,1},{3,4},{4,3},{5,6},{6,5},{7,8},{8,7},{9,10},{10,... | collective-permute-start | bytes 24584 | tf_op jit(solution)/shard_map/ppermute | solution.py:552
  6.7 6.1 %collective-permute-start = (f32[16,128]{1,0:T(8,128)}, f32[16,128]{1,0:T(8,128)S(1)}, u32[]{:S(2)}, u32[]{:S(2)}) collective-permute-start(f32[16,128]{1,0:T(8,128)} %shard_map.212), channel_id=1, source_target_pairs={{0,1},{1,0},{2,3},{3,2},{4,5},{5,4},{6,7},{7,6},{8,9},{9,8},{10,11... | collective-permute-start | bytes 24584 | tf_op jit(solution)/shard_map/ppermute | solution.py:552
  12.8 0.0 collective-permute-done.1
  12.9 1.0 %collective-permute-done = f32[16,128]{1,0:T(8,128)S(1)} collective-permute-done((f32[16,128]{1,0:T(8,128)}, f32[16,128]{1,0:T(8,128)S(1)}, u32[]{:S(2)}, u32[]{:S(2)}) %collective-permute-start) | collective-permute-done | bytes 8224 | tf_op jit(solution)/shard_map/ppermute | solution.py:552
  13.8 0.0 copy-start.1
  13.8 0.7 %copy-done.1 = f32[16,128]{1,0:T(8,128)S(1)} copy-done((f32[16,128]{1,0:T(8,128)S(1)}, f32[16,128]{1,0:T(8,128)}, u32[]{:S(2)}) %copy-start.1) | copy-done | bytes 8216
  14.5 0.0 copy-start
  14.5 10.7 %collective-permute-start.3 = (f32[16,256]{1,0:T(8,128)S(1)}, f32[16,256]{1,0:T(8,128)S(1)}, u32[]{:S(2)}, u32[]{:S(2)}) collective-permute-start(f32[16,256]{1,0:T(8,128)S(1)} %pad_maximum_fusion.mid), channel_id=1, source_target_pairs={{0,496},{16,32},{32,16},{48,64},{64,48},{80,96},{96,80},{112,128},... | collective-permute-start | bytes 49160 | tf_op jit(solution)/shard_map/ppermute | solution.py:552
  25.2 1.9 %collective-permute-start.2 = (f32[16,256]{1,0:T(8,128)S(1)}, f32[16,256]{1,0:T(8,128)S(1)}, u32[]{:S(2)}, u32[]{:S(2)}) collective-permute-start(f32[16,256]{1,0:T(8,128)S(1)} %pad_maximum_fusion.mid), channel_id=1, source_target_pairs={{0,16},{16,0},{32,48},{48,32},{64,80},{80,64},{96,112},{112,96},{1... | collective-permute-start | bytes 49160 | tf_op jit(solution)/shard_map/ppermute | solution.py:552
  27.2 0.0 collective-permute-done.3.near_b
  27.2 0.0 copy-start.2
  27.2 2.5 %collective-permute-done.2.near_a = f32[16,256]{1,0:T(8,128)S(1)} collective-permute-done((f32[16,256]{1,0:T(8,128)S(1)}, f32[16,256]{1,0:T(8,128)S(1)}, u32[]{:S(2)}, u32[]{:S(2)}) %collective-permute-start.2) | collective-permute-done | bytes 16416 | tf_op jit(solution)/shard_map/ppermute | solution.py:552
  29.7 0.0 copy-start.3
  29.7 0.0 copy-done
  29.7 0.0 copy-done.2
  29.7 0.6 %copy-done.3 = f32[16,256]{1,0:T(8,128)} copy-done((f32[16,256]{1,0:T(8,128)}, f32[16,256]{1,0:T(8,128)S(1)}, u32[]{:S(2)}) %copy-start.3) | copy-done | bytes 16408
  30.3 22.4 %shard_map.213 = (f32[3,1,128]{2,1,0:T(1,128)}, f32[1,128]{1,0:T(1,128)}) custom-call(s32[1]{0:T(128)} %bitcast.odd, f32[16,256]{1,0:T(8,128)} %copy-done, f32[16,256]{1,0:T(8,128)} %copy-done.3, f32[16,256]{1,0:T(8,128)} %copy-done.2, s32[8,512]{1,0:T(8,128)} %constant.56.clone.atom_table_hbm, s32[8,1408]{1,0:T(8,128)} %constant.57.clone.edge_table_hbm, ...), custom_call_target="tpu_custom_call" | custom-call | tf_op jit(solution)/shard_map/pallas_call | solution.py:624
  (4 shorter events, 0.0 us)
Async XLA Ops:
  2.1 10.7 %collective-permute-start.1 = (f32[16,128]{1,0:T(8,128)}, f32[16,128]{1,0:T(8,128)S(1)}, u32[]{:S(2)}, u32[]{:S(2)}) collective-permute-start(f32[16,128]{1,0:T(8,128)} %shard_map.212), channel_id=1, source_target_pairs={{0,15},{1,2},{2,1},{3,4},{4,3},{5,6},{6,5},{7,8},{8,7},{9,10},{10,... | collective-permute-start | bytes 24584 | tf_op jit(solution)/shard_map/ppermute | solution.py:552
  6.7 7.1 %collective-permute-start = (f32[16,128]{1,0:T(8,128)}, f32[16,128]{1,0:T(8,128)S(1)}, u32[]{:S(2)}, u32[]{:S(2)}) collective-permute-start(f32[16,128]{1,0:T(8,128)} %shard_map.212), channel_id=1, source_target_pairs={{0,1},{1,0},{2,3},{3,2},{4,5},{5,4},{6,7},{7,6},{8,9},{9,8},{10,11... | collective-permute-start | bytes 24584 | tf_op jit(solution)/shard_map/ppermute | solution.py:552
  13.8 0.7 %copy-start.1 = (f32[16,128]{1,0:T(8,128)S(1)}, f32[16,128]{1,0:T(8,128)}, u32[]{:S(2)}) copy-start(f32[16,128]{1,0:T(8,128)} %shard_map.212) | copy-start | bytes 24580
  14.5 15.2 %copy-start = (f32[16,256]{1,0:T(8,128)}, f32[16,256]{1,0:T(8,128)S(1)}, u32[]{:S(2)}) copy-start(f32[16,256]{1,0:T(8,128)S(1)} %pad_maximum_fusion.mid) | copy-start | bytes 49156
  14.5 12.6 %collective-permute-start.3 = (f32[16,256]{1,0:T(8,128)S(1)}, f32[16,256]{1,0:T(8,128)S(1)}, u32[]{:S(2)}, u32[]{:S(2)}) collective-permute-start(f32[16,256]{1,0:T(8,128)S(1)} %pad_maximum_fusion.mid), channel_id=1, source_target_pairs={{0,496},{16,32},{32,16},{48,64},{64,48},{80,96},{96,80},{112,128},... | collective-permute-start | bytes 49160 | tf_op jit(solution)/shard_map/ppermute | solution.py:552
  25.2 4.5 %collective-permute-start.2 = (f32[16,256]{1,0:T(8,128)S(1)}, f32[16,256]{1,0:T(8,128)S(1)}, u32[]{:S(2)}, u32[]{:S(2)}) collective-permute-start(f32[16,256]{1,0:T(8,128)S(1)} %pad_maximum_fusion.mid), channel_id=1, source_target_pairs={{0,16},{16,0},{32,48},{48,32},{64,80},{80,64},{96,112},{112,96},{1... | collective-permute-start | bytes 49160 | tf_op jit(solution)/shard_map/ppermute | solution.py:552
  27.2 2.5 %copy-start.2 = (f32[16,256]{1,0:T(8,128)}, f32[16,256]{1,0:T(8,128)S(1)}, u32[]{:S(2)}) copy-start(f32[16,256]{1,0:T(8,128)S(1)} %collective-permute-done.3.near_b) | copy-start | bytes 49156
  29.7 0.6 %copy-start.3 = (f32[16,256]{1,0:T(8,128)}, f32[16,256]{1,0:T(8,128)S(1)}, u32[]{:S(2)}) copy-start(f32[16,256]{1,0:T(8,128)S(1)} %collective-permute-done.2.near_a) | copy-start | bytes 49156

commit v2 on v1

--- a/solution.py
+++ b/solution.py
@@ -91,6 +91,26 @@
 
 def dot3(a, b):
     return dots(split(a), split(b))
+
+
+def wide(w_t):
+    high = rounded(w_t)
+    return jnp.concatenate([high, high, w_t - high], 0).T.astype(BF16)
+
+
+def wide_rows(w):
+    high, low = split(w)
+    return jnp.concatenate([high, high, low], 1)
+
+
+def tall(x):
+    high, low = split(x)
+    return jnp.concatenate([high, low, high], 0)
+
+
+def tall_small(x):
+    high = rounded(x)
+    return jnp.concatenate([high, x - high, high], 0).astype(BF16)
 
 
 def silu_pair(x):
@@ -174,6 +194,11 @@
     square_grad,
     shape_grad,
     radial_grad,
+    slopes,
+    stack,
+    left_ref,
+    grad_ref,
+    raw_ref,
     atom_table,
     edge_table,
     embedding,
@@ -271,16 +296,27 @@
         plain = column_of(atom_table[5:6, cut].astype(F32))
         listed = column_of(key_b[c])
         for e in range(TILES):
-            if e < 3 and c > 1:
+            if (e < 3 and c > 1) or (e > 6 and c == 0):
                 continue
+            if e == 6 and c == 0:
+                hot1[cut, 384:512] = jnp.zeros((128, 128), BF16)
+                continue
+            few = c == 3 and e < 7
             wanted = key[:, 128 * e : 128 * e + 128]
-            hit = jnp.where((plain == wanted) | (listed == wanted), 1.0, 0.0).astype(BF16)
+            rows = 16 if few else 128
+            if c == 0 or e < 3:
+                found = (plain if c == 0 and e < 3 else listed) == wanted
+            else:
+                found = (plain[0:rows] == wanted) | (listed[0:rows] == wanted)
+            hit = jnp.where(found, 1.0, 0.0).astype(BF16)
+            if few:
+                hit = jnp.concatenate([hit, jnp.zeros((112, 128), BF16)], 0)
             if e < 3:
                 hot0[cut, 128 * e : 128 * e + 128] = hit
             elif e < 7:
                 hot1[cut, 128 * (e - 3) : 128 * (e - 3) + 128] = hit
             else:
-                hot2[cut, 128 * (e - 7) : 128 * (e - 7) + 128] = hit
+                hot2[128 * c - 128 : 128 * c, 128 * (e - 7) : 128 * (e - 7) + 128] = hit
 
     raw = jnp.concatenate([t[0:8] for t in atom_tiles], 1)
     first = rounded(raw)
@@ -288,12 +324,12 @@
     third = rounded(raw - first - second)
     terms = jnp.concatenate([first, second, third, third], 0).astype(BF16)
     found = jnp.concatenate(
-        [mm(terms[:, 0:256], hot0[...]), mm(terms, hot1[...]), mm(terms, hot2[...])], 1
+        [mm(terms[:, 0:256], hot0[...]), mm(terms, hot1[...]), mm(terms[:, 128:512], hot2[...])], 1
     )
     found = found[0:8] + found[8:16] + found[16:24]
     away = [found[i : i + 1] - receivers[i : i + 1] for i in range(3)]
     spec_row[0:1, :] = found[3:4]
-    spec_row[1:2, :] = live
+    spec_row[1:2, :] = live * (1.0 / 3.0)
 
     radius_sq = away[0] * away[0] + away[1] * away[1] + away[2] * away[2] + SOFTEN
     radius = jnp.sqrt(radius_sq)
@@ -356,75 +392,97 @@
 
     lax.fori_loop(0, TILES, embed_edges, 0)
 
-    basis_s = split(basis)
-    pre1 = dots(split(in_one[...].T), basis_s)
-    hid1, dhid1 = silu_pair(pre1)
-    pre1 = dots(split(mid_one[...]), split(hid1))
-    top1, dtop1 = silu_pair(pre1)
-    dhid1, dtop1 = dhid1[:, near], dtop1[:, near]
-    top1 = split(top1)
+    def out_parts(weight):
+        return [wide(weight[:, 128 * g : 128 * g + 128]) for g in range(3)]
+
+    net_one = (wide(in_one[...]), wide(mid_one[...].T), out_parts(out_one))
+    net_two = (wide(in_two[...]), wide(mid_two[...].T), out_parts(out_two))
+    chunks = [slice(i, min(i + 256, EDGES)) for i in range(0, EDGES, 256)]
+    chunks_two = [slice(i, min(i + 256, EDGES_TWO)) for i in range(0, EDGES_TWO, 256)]
+    jobs = [(net_one, c, 0) for c in chunks] + [(net_two, c, 1) for c in chunks_two]
+
+    def layer(weight, source, chunk, slot, keep):
+        value, slope_here = silu_pair(mm(weight, source))
+        if chunk.start < EDGES_BACK:
+            slopes[keep, :, chunk] = slope_here
+        stack[slot, :, chunk] = tall(value)
+
+    for net, chunk, slot in jobs:
+        layer(net[0], tall_small(basis[:, chunk]), chunk, slot, 2 * slot)
+    for net, chunk, slot in jobs:
+        layer(net[1], stack[slot, :, chunk], chunk, slot, 2 * slot + 1)
+    for net, chunk, slot in jobs:
+        for g in range(3):
+            weight = mm(net[2][g], stack[slot, :, chunk])
+            if slot:
+                w_two[g, :, chunk] = weight
+            else:
+                carried[g, :, chunk] = weight * emb_edge[:, chunk]
+
     for g in range(3):
-        weight = dots(split(out_one[:, 128 * g : 128 * g + 128].T), top1)
-        carried[g] = weight * emb_edge[...]
-    basis_two = (basis_s[0][:, 0:EDGES_TWO], basis_s[1][:, 0:EDGES_TWO])
-    pre2 = dots(split(in_two[...].T), basis_two)
-    hid2, dhid2 = silu_pair(pre2)
-    pre2 = dots(split(mid_two[...]), split(hid2))
-    top2, dtop2 = silu_pair(pre2)
-    dhid2, dtop2 = dhid2[:, near], dtop2[:, near]
-    top2 = split(top2)
-    for g in range(3):
-        w_two[g] = dots(split(out_two[:, 128 * g : 128 * g + 128].T), top2)
-
-    for g in range(3):
-        high, low = split(mixing[g])
-        mix_split[g, 0:128, :] = high
-        mix_split[g, 128:256, :] = low
-        high, low = split(mixing[g].T)
-        mix_back[g, 0:128, :] = high
-        mix_back[g, 128:256, :] = low
+        mix_split[g] = wide_rows(mixing[g])
+        mix_back[g] = wide_rows(mixing[g].T)
 
     def degree(m):
-        return (m > 0).astype(jnp.int32) + (m > 3).astype(jnp.int32)
-
-    def moment(m, g):
-        y = shape_row[pl.ds(m, 1), :]
+        return int(m > 0) + int(m > 3)
+
+    def moment(m, half):
+        g = degree(m)
+        y = shape_row[m : m + 1, :]
 
         def part(e):
             at = slice(128 * e, 128 * e + 128)
-            return carried[g, :, at] * y[:, at]
-
-        tail = part(10)
-        value = jnp.concatenate(
-            [
-                part(0) + part(1) + part(2),
-                part(3) + part(4) + part(5),
-                part(7) + part(8) + part(9),
-                tail + roll_up(tail, 8) + roll_up(tail, 16),
-            ],
-            1,
-        ) * (1.0 / 3.0)
-        moments[m] = value
-        high, low = split(value)
-        both = mm(mix_split[g], high)
-        mixed = both[0:128] + both[128:256] + mm(mix_split[g, 0:128, :], low)
-        return value, mixed
-
-    value, mixed = moment(0, 0)
-    squares[...] = value * value
-    scalar_feat[...] = mixed
-
-    def moment_step(m, carry):
-        value, mixed = moment(m, degree(m))
-        squares[...] += value * value
-        high, low = split(mixed)
-        feats[m, 0:128, :] = high
-        feats[m, 128:256, :] = low
-        return carry
-
-    lax.fori_loop(1, 9, moment_step, 0)
+            return carried[g, :, at] * y[:, at] if m else carried[g, :, at]
+
+        if half == 0:
+            one = part(0) + part(1) + part(2)
+            two = part(3) + part(4) + part(5)
+        else:
+            one = part(7) + part(8) + part(9)
+            two = part(10)
+            two = two + roll_up(two, 8) + roll_up(two, 16)
+        at = slice(256 * half, 256 * half + 256)
+        value = jnp.concatenate([one, two], 1)
+        moments[m, :, at] = value
+        if m:
+            squares[:, at] += value * value
+        else:
+            squares[:, at] = value * value
+        mixed = mm(mix_split[g], tall(value))
+        if m:
+            high, low = split(mixed)
+            feats[m, 0:128, at] = high
+            feats[m, 128:256, at] = low
+        else:
+            scalar_feat[:, at] = mixed
+
+    def gather(m, at, first):
+        g = degree(m)
+        y = shape_row[m : m + 1, :]
+        if at.start < 384:
+            part = mm(feats[m, :, 0:256], hot0[:, at])
+        else:
+            part = mm(feats[m], hot1[:, at.start - 384 : at.stop - 384])
+        part = part[0:128] + part[128:256]
+        gathered_ref[m, :, at] = part
+        if m:
+            part = part * y[:, at]
+        if first:
+            proj[g, :, at] = part
+        else:
+            proj[g, :, at] += part
+
+    spans = (slice(0, 256), slice(256, 384), slice(384, 640), slice(640, 896))
+    for m in range(9):
+        for half in range(2):
+            moment(m, half)
+            if m > 1:
+                for at in spans[2 * half : 2 * half + 2]:
+                    gather(m - 1, at, m - 1 in (1, 4))
+    for at in spans[0:2]:
+        gather(8, at, False)
     element_rows = jnp.concatenate([t[3:4] for t in atom_tiles], 1)
-    scalar = scalar_feat[...] + dot3(square_mix[...], squares[...])
+    scalar = scalar_feat[...] + mm(wide_rows(square_mix[...]), tall(squares[...]))
     scalar = scalar + jnp.concatenate(
         [element(element_rows[:, 128 * t : 128 * t + 128]) for t in range(4)], 1
     )
@@ -432,25 +490,12 @@
     high, low = split(scalar)
     feats[0, 0:128, :] = high
     feats[0, 128:256, :] = low
-
-    proj[...] = jnp.zeros_like(proj)
-
-    def gather_step(m, carry):
-        g = degree(m)
-        left = feats[m]
-        part = mm(left[:, 0:256], hot0[...])
-        rest = mm(left, hot1[...])
-        part = part[0:128] + part[128:256]
-        rest = rest[0:128] + rest[128:256]
-        gathered_ref[m, :, 0:384] = part
-        gathered_ref[m, :, 384:896] = rest
-        y = shape_row[pl.ds(m, 1), :]
-        proj[g, :, 0:384] += part * y[:, 0:384]
-        proj[g, :, 384:896] += rest * y[:, 384:896]
-        return carry
-
-    lax.fori_loop(0, 9, gather_step, 0)
-    live_two = live[:, 0:EDGES_TWO]
+    for at in spans[2:4]:
+        gather(8, at, False)
+    for at in spans:
+        gather(0, at, True)
+
+    live_two = live[:, 0:EDGES_TWO] * (1.0 / 3.0)
     term = (w_two[0] * proj[0] + w_two[1] * proj[1] + w_two[2] * proj[2]) * live_two
     tail = term[:, 768:896]
     total = jnp.concatenate(
@@ -460,9 +505,9 @@
             tail + roll_up(tail, 32) + roll_up(tail, 64),
         ],
         1,
-    ) * (1.0 / 3.0)
-    refined = dot3(mix_two[...], total) + scalar_feat[:, 0:384]
-    hidden = dot3(read_hidden[...], refined)
+    )
+    refined = mm(wide_rows(mix_two[...]), tall(total)) + scalar_feat[:, 0:384]
+    hidden = mm(wide_rows(read_hidden[...]), tall(refined))
     act, dact = silu_pair(hidden)
     out_column = jnp.broadcast_to(column_of(read_out[...])[:, 0:1], (16, 384))
     one_column = column_of(readout_one[...])
@@ -472,8 +517,8 @@
         + pair_own
     )
 
-    refined_grad = dot3(read_hidden[...].T, dact * out_column)
-    total_grad = dot3(mix_two[...].T, refined_grad) * (1.0 / 3.0)
+    refined_grad = mm(wide(read_hidden[...]), tall(dact * out_column))
+    total_grad = mm(wide_rows(mix_two[...].T), tall(refined_grad))
     lane128 = lax.broadcasted_iota(jnp.int32, (128, 128), 1)
     tail = jnp.where(lane128 < 32, total_grad[:, 256:384], 0.0)
     tail = tail + pltpu.roll(tail, 32, 1) + pltpu.roll(tail, 64, 1)
@@ -482,46 +527,78 @@
     for g in range(3):
         queue[g] = term_grad * w_two[g]
         proj[g, :, near] = term_grad[:, near] * proj[g, :, near]
-    radial_grad[...] = jnp.zeros_like(radial_grad)
-
-    def back(m, g, first):
-        y = shape_row[pl.ds(m, 1), :]
-        q = queue[g]
-        high, low = split(q * y[:, 0:EDGES_TWO])
-        left = jnp.concatenate([high, low], 0)
-        grad = mm_nt(left[:, 0:384], hot0[...]) + mm_nt(left[:, 384:896], hot1[0:256, :])
-        grad = grad[0:128] + grad[128:256]
-        if first:
+    def spread_edges(m):
+        g = degree(m)
+        y = shape_row[m : m + 1, :]
+        for row in range(0, 128, 16):
+            rows = slice(row, row + 16)
+            part = queue[g, rows, :]
+            high, low = split(part * y[:, 0:EDGES_TWO] if m else part)
+            left_ref[m % 3, rows, :] = high
+            left_ref[m % 3, 128 + row : 144 + row, :] = low
+
+    def scatter(m):
+        grad = mm_nt(left_ref[m % 3, :, 0:384], hot0[...])
+        grad = grad + mm_nt(left_ref[m % 3, :, 384:896], hot1[0:256, :])
+        raw_ref[m % 3] = grad[0:128] + grad[128:256]
+
+    def unmix(m):
+        grad = raw_ref[m % 3]
+        if m == 0:
             grad = grad + refined_grad[:, 0:256] + jnp.concatenate([one_column] * 2, 1)
-            square_grad[...] = 2.0 * dot3(square_mix[...].T, grad)
-        high, low = split(grad)
-        both = mm(mix_back[g], high)
-        grad = both[0:128] + both[128:256] + mm(mix_back[g, 0:128, :], low)
-        grad = (grad + square_grad[...] * moments[m, :, 0:256]) * (1.0 / 3.0)
-        wide = jnp.concatenate([grad[:, 0:128]] * 3 + [grad[:, 128:256]] * 3, 1)
-        both = q[:, near] * gathered_ref[m, :, near] + wide * carried[g, :, near]
-        shape_grad[pl.ds(m, 1), :] = jnp.sum(both, axis=0, keepdims=True)
-        radial_grad[g] += wide * y[:, near]
-
-    back(0, 0, True)
-
-    def back_step(m, carry):
-        back(m, degree(m), False)
-        return carry
-
-    lax.fori_loop(1, 9, back_step, 0)
-
-    def radial_back(grads, weight_out, weight_mid, weight_in, dtop, dhid):
-        top_grad = 0.0
-        for g in range(3):
-            top_grad = top_grad + dot3(weight_out[:, 128 * g : 128 * g + 128], grads[g])
-        hid_grad = dot3(weight_mid[...].T, top_grad * dtop)
-        return dot3(weight_in[...], hid_grad * dhid)
-
-    ones = [radial_grad[g] * emb_edge[:, near] for g in range(3)]
-    basis_grad = radial_back(ones, out_one, mid_one, in_one, dtop1, dhid1)
-    twos = [proj[g, :, near] for g in range(3)]
-    basis_grad = basis_grad + radial_back(twos, out_two, mid_two, in_two, dtop2, dhid2)
+            square_grad[...] = 2.0 * mm(wide_rows(square_mix[...].T), tall(grad))
+        grad = mm(mix_back[degree(m)], tall(grad))
+        grad_ref[m % 3] = grad + square_grad[...] * moments[m, :, 0:256]
+
+    def edge_parts(m, start, total):
+        g = degree(m)
+        y = shape_row[m : m + 1, :]
+        for row in range(start, start + 64, 8):
+            rows = slice(row, row + 8)
+            here = grad_ref[m % 3, rows, :]
+            here = jnp.concatenate([here[:, 0:128]] * 3 + [here[:, 128:256]] * 3, 1)
+            both = queue[g, rows, near] * gathered_ref[m, rows, near]
+            both = both + here * carried[g, rows, near]
+            total = both if total is None else total + both
+            here = here * y[:, near] if m else here
+            if m in (0, 1, 4):
+                radial_grad[g, rows, :] = here
+            else:
+                radial_grad[g, rows, :] += here
+        return total
+
+    for step in range(11):
+        total = None
+        if step < 9:
+            spread_edges(step)
+            scatter(step)
+        if step > 1:
+            total = edge_parts(step - 2, 0, None)
+        if 0 < step < 10:
+            unmix(step - 1)
+        if step > 1:
+            total = edge_parts(step - 2, 64, total)
+            shape_grad[step - 2 : step - 1, :] = jnp.sum(total, axis=0, keepdims=True)
+
+    back_one = (jnp.concatenate(split(out_one[...]), 0), wide(mid_one[...]), wide(in_one[...].T))
+    back_two = (jnp.concatenate(split(out_two[...]), 0), wide(mid_two[...]), wide(in_two[...].T))
+
+    def network_back(weights, grads, chunk, slot):
+        high, low = split(jnp.concatenate(grads, 0))
+        top_grad = mm(weights[0], high)
+        top_grad = top_grad[0:64] + top_grad[64:128] + mm(weights[0][0:64], low)
+        hid_grad = mm(weights[1], tall(top_grad * slopes[slot + 1, :, chunk]))
+        return mm(weights[2], tall(hid_grad * slopes[slot, :, chunk]))
+
+    parts = []
+    for start in range(0, EDGES_BACK, 256):
+        chunk = slice(start, start + 256)
+        ones = [radial_grad[g, :, chunk] * emb_edge[:, chunk] for g in range(3)]
+        twos = [proj[g, :, chunk] for g in range(3)]
+        parts.append(
+            network_back(back_one, ones, chunk, 0) + network_back(back_two, twos, chunk, 2)
+        )
+    basis_grad = jnp.concatenate(parts, 1)
 
     ux, uy, uz, inverse = ux[:, near], uy[:, near], uz[:, near], inverse[:, near]
     ym = [shape_grad[m : m + 1, :] for m in range(9)]
@@ -634,7 +711,7 @@
         scratch_shapes=[
             pltpu.VMEM((256, 384), BF16),
             pltpu.VMEM((512, 512), BF16),
-            pltpu.VMEM((512, 512), BF16),
+            pltpu.VMEM((384, 512), BF16),
             pltpu.VMEM((5, 128, 128), F32),
             pltpu.VMEM((8, EDGES), F32),
             pltpu.VMEM((128, EDGES), F32),
@@ -646,13 +723,18 @@
             pltpu.VMEM((9, 256, 512), BF16),
             pltpu.VMEM((9, 128, EDGES_TWO), F32),
             pltpu.VMEM((3, 128, EDGES_TWO), F32),
-            pltpu.VMEM((3, 256, 128), BF16),
-            pltpu.VMEM((3, 256, 128), BF16),
+            pltpu.VMEM((3, 128, 384), BF16),
+            pltpu.VMEM((3, 128, 384), BF16),
             pltpu.VMEM((3, 128, EDGES_TWO), F32),
             pltpu.VMEM((3, 128, EDGES_TWO), F32),
             pltpu.VMEM((128, 256), F32),
             pltpu.VMEM((16, EDGES_BACK), F32),
             pltpu.VMEM((3, 128, EDGES_BACK), F32),
+            pltpu.VMEM((4, 64, EDGES_BACK), F32),
+            pltpu.VMEM((2, 192, EDGES), BF16),
+            pltpu.VMEM((3, 256, EDGES_TWO), BF16),
+            pltpu.VMEM((3, 128, 256), F32),
+            pltpu.VMEM((3, 128, 256), F32),
         ]
         + [pltpu.VMEM(h.shape, h.dtype) for h in held]
         + [pltpu.SemaphoreType.DMA((len(held),))],

time: 53.2 us -> 44.3 us (0.83)
  Pallas kernels: 23.9 us -> 14.9 us
    pallas_call x1, Pallas kernels: 22.4 us -> 13.4 us  [local(): pl.pallas_call(main_kernel, out_shape=(jax.ShapeDtypeStruct((3, 1, 128),...]
where the time goes in v2:
time: 44.3 us; the launch traced here: 43.7 us
  starting transfers between devices  23.3 us (53%)
  Pallas kernels  14.9 us (34%)
  waiting for transfers between devices  3.5 us (8%)
  local copies, waits for them, and re-layouts  1.29 us (3%)
  between operations  0.73 us (2%)
    ppermute x4, starting transfers between devices, swap(): return lax.ppermute(value, axis, pairs)  23.3 us
    pallas_call x1, Pallas kernels, local(): pl.pallas_call(main_kernel, out_shape=(jax.ShapeDtypeStruct((3, 1, 128),...  13.4 us
    ppermute x4, waiting for transfers between devices, swap(): return lax.ppermute(value, axis, pairs)  3.5 us
    pallas_call x1, Pallas kernels, local(): pl.pallas_call(pack_kernel, out_shape=jax.ShapeDtypeStruct((16, 128), F32...  1.49 us
    unnamed x8, local copies, waits for them, and re-layouts  1.29 us
  transfers between devices with their start and end apart: 4, of which 2 were waited for; matrix products, arithmetic and copies ran while one was open for 0% of the time, Pallas kernels for 0%

profile of v2, /device:TPU:1, one launch (start us, length us, event | category | flops | bytes accessed | tf_op | source)
XLA Modules:
  0.0 43.7 jit_solution(15617238932801675333)
XLA Ops:
  0.6 1.5 %shard_map.212 = f32[16,128]{1,0:T(8,128)} custom-call(f32[3,1,128]{2,1,0:T(1,128)} %bitcast.23, s32[1,128]{1,0:T(1,128)} %bitcast.28, s32[3,1,128]{2,1,0:T(1,128)} %bitcast.24, s32[1,128]{1,0:T(1,128)} %bitcast.29, s32[3,1,128]{2,1,0:T(1,128)} %bitcast.25, s32[1,64]{1,0:T(1,128)} %bitcast.30), custom_call_target="tpu_custom_call" | custom-call | tf_op jit(solution)/shard_map/pallas_call | solution.py:653
  2.1 4.6 %collective-permute-start.1 = (f32[16,128]{1,0:T(8,128)}, f32[16,128]{1,0:T(8,128)S(1)}, u32[]{:S(2)}, u32[]{:S(2)}) collective-permute-start(f32[16,128]{1,0:T(8,128)} %shard_map.212), channel_id=1, source_target_pairs={{0,15},{1,2},{2,1},{3,4},{4,3},{5,6},{6,5},{7,8},{8,7},{9,10},{10,... | collective-permute-start | bytes 24584 | tf_op jit(solution)/shard_map/ppermute | solution.py:629
  6.7 6.1 %collective-permute-start = (f32[16,128]{1,0:T(8,128)}, f32[16,128]{1,0:T(8,128)S(1)}, u32[]{:S(2)}, u32[]{:S(2)}) collective-permute-start(f32[16,128]{1,0:T(8,128)} %shard_map.212), channel_id=1, source_target_pairs={{0,1},{1,0},{2,3},{3,2},{4,5},{5,4},{6,7},{7,6},{8,9},{9,8},{10,11... | collective-permute-start | bytes 24584 | tf_op jit(solution)/shard_map/ppermute | solution.py:629
  12.8 0.0 collective-permute-done.1
  12.9 1.0 %collective-permute-done = f32[16,128]{1,0:T(8,128)S(1)} collective-permute-done((f32[16,128]{1,0:T(8,128)}, f32[16,128]{1,0:T(8,128)S(1)}, u32[]{:S(2)}, u32[]{:S(2)}) %collective-permute-start) | collective-permute-done | bytes 8224 | tf_op jit(solution)/shard_map/ppermute | solution.py:629
  13.8 0.0 copy-start.1
  13.8 0.7 %copy-done.1 = f32[16,128]{1,0:T(8,128)S(1)} copy-done((f32[16,128]{1,0:T(8,128)S(1)}, f32[16,128]{1,0:T(8,128)}, u32[]{:S(2)}) %copy-start.1) | copy-done | bytes 8216
  14.5 0.0 copy-start
  14.5 10.7 %collective-permute-start.3 = (f32[16,256]{1,0:T(8,128)S(1)}, f32[16,256]{1,0:T(8,128)S(1)}, u32[]{:S(2)}, u32[]{:S(2)}) collective-permute-start(f32[16,256]{1,0:T(8,128)S(1)} %pad_maximum_fusion.mid), channel_id=1, source_target_pairs={{0,496},{16,32},{32,16},{48,64},{64,48},{80,96},{96,80},{112,128},... | collective-permute-start | bytes 49160 | tf_op jit(solution)/shard_map/ppermute | solution.py:629
  25.2 1.9 %collective-permute-start.2 = (f32[16,256]{1,0:T(8,128)S(1)}, f32[16,256]{1,0:T(8,128)S(1)}, u32[]{:S(2)}, u32[]{:S(2)}) collective-permute-start(f32[16,256]{1,0:T(8,128)S(1)} %pad_maximum_fusion.mid), channel_id=1, source_target_pairs={{0,16},{16,0},{32,48},{48,32},{64,80},{80,64},{96,112},{112,96},{1... | collective-permute-start | bytes 49160 | tf_op jit(solution)/shard_map/ppermute | solution.py:629
  27.2 0.0 collective-permute-done.3.near_b
  27.2 0.0 copy-start.2
  27.2 2.5 %collective-permute-done.2.near_a = f32[16,256]{1,0:T(8,128)S(1)} collective-permute-done((f32[16,256]{1,0:T(8,128)S(1)}, f32[16,256]{1,0:T(8,128)S(1)}, u32[]{:S(2)}, u32[]{:S(2)}) %collective-permute-start.2) | collective-permute-done | bytes 16416 | tf_op jit(solution)/shard_map/ppermute | solution.py:629
  29.7 0.0 copy-start.3
  29.7 0.0 copy-done
  29.7 0.0 copy-done.2
  29.7 0.6 %copy-done.3 = f32[16,256]{1,0:T(8,128)} copy-done((f32[16,256]{1,0:T(8,128)}, f32[16,256]{1,0:T(8,128)S(1)}, u32[]{:S(2)}) %copy-start.3) | copy-done | bytes 16408
  30.3 13.4 %shard_map.213 = (f32[3,1,128]{2,1,0:T(1,128)}, f32[1,128]{1,0:T(1,128)}) custom-call(s32[1]{0:T(128)} %bitcast.odd, f32[16,256]{1,0:T(8,128)} %copy-done, f32[16,256]{1,0:T(8,128)} %copy-done.3, f32[16,256]{1,0:T(8,128)} %copy-done.2, s32[8,512]{1,0:T(8,128)} %constant.56.clone.atom_table_hbm, s32[8,1408]{1,0:T(8,128)} %constant.57.clone.edge_table_hbm, ...), custom_call_target="tpu_custom_call" | custom-call | tf_op jit(solution)/shard_map/pallas_call | solution.py:701
  (4 shorter events, 0.0 us)
Async XLA Ops:
  2.1 10.7 %collective-permute-start.1 = (f32[16,128]{1,0:T(8,128)}, f32[16,128]{1,0:T(8,128)S(1)}, u32[]{:S(2)}, u32[]{:S(2)}) collective-permute-start(f32[16,128]{1,0:T(8,128)} %shard_map.212), channel_id=1, source_target_pairs={{0,15},{1,2},{2,1},{3,4},{4,3},{5,6},{6,5},{7,8},{8,7},{9,10},{10,... | collective-permute-start | bytes 24584 | tf_op jit(solution)/shard_map/ppermute | solution.py:629
  6.7 7.1 %collective-permute-start = (f32[16,128]{1,0:T(8,128)}, f32[16,128]{1,0:T(8,128)S(1)}, u32[]{:S(2)}, u32[]{:S(2)}) collective-permute-start(f32[16,128]{1,0:T(8,128)} %shard_map.212), channel_id=1, source_target_pairs={{0,1},{1,0},{2,3},{3,2},{4,5},{5,4},{6,7},{7,6},{8,9},{9,8},{10,11... | collective-permute-start | bytes 24584 | tf_op jit(solution)/shard_map/ppermute | solution.py:629
  13.8 0.7 %copy-start.1 = (f32[16,128]{1,0:T(8,128)S(1)}, f32[16,128]{1,0:T(8,128)}, u32[]{:S(2)}) copy-start(f32[16,128]{1,0:T(8,128)} %shard_map.212) | copy-start | bytes 24580
  14.5 15.2 %copy-start = (f32[16,256]{1,0:T(8,128)}, f32[16,256]{1,0:T(8,128)S(1)}, u32[]{:S(2)}) copy-start(f32[16,256]{1,0:T(8,128)S(1)} %pad_maximum_fusion.mid) | copy-start | bytes 49156
  14.5 12.6 %collective-permute-start.3 = (f32[16,256]{1,0:T(8,128)S(1)}, f32[16,256]{1,0:T(8,128)S(1)}, u32[]{:S(2)}, u32[]{:S(2)}) collective-permute-start(f32[16,256]{1,0:T(8,128)S(1)} %pad_maximum_fusion.mid), channel_id=1, source_target_pairs={{0,496},{16,32},{32,16},{48,64},{64,48},{80,96},{96,80},{112,128},... | collective-permute-start | bytes 49160 | tf_op jit(solution)/shard_map/ppermute | solution.py:629
  25.2 4.5 %collective-permute-start.2 = (f32[16,256]{1,0:T(8,128)S(1)}, f32[16,256]{1,0:T(8,128)S(1)}, u32[]{:S(2)}, u32[]{:S(2)}) collective-permute-start(f32[16,256]{1,0:T(8,128)S(1)} %pad_maximum_fusion.mid), channel_id=1, source_target_pairs={{0,16},{16,0},{32,48},{48,32},{64,80},{80,64},{96,112},{112,96},{1... | collective-permute-start | bytes 49160 | tf_op jit(solution)/shard_map/ppermute | solution.py:629
  27.2 2.5 %copy-start.2 = (f32[16,256]{1,0:T(8,128)}, f32[16,256]{1,0:T(8,128)S(1)}, u32[]{:S(2)}) copy-start(f32[16,256]{1,0:T(8,128)S(1)} %collective-permute-done.3.near_b) | copy-start | bytes 49156
  29.7 0.6 %copy-start.3 = (f32[16,256]{1,0:T(8,128)}, f32[16,256]{1,0:T(8,128)S(1)}, u32[]{:S(2)}) copy-start(f32[16,256]{1,0:T(8,128)S(1)} %collective-permute-done.2.near_a) | copy-start | bytes 49156

commit v3 on v2

--- a/solution.py
+++ b/solution.py
@@ -199,6 +199,7 @@
     left_ref,
     grad_ref,
     raw_ref,
+    square_back,
     atom_table,
     edge_table,
     embedding,
@@ -421,7 +422,6 @@
 
     for g in range(3):
         mix_split[g] = wide_rows(mixing[g])
-        mix_back[g] = wide_rows(mixing[g].T)
 
     def degree(m):
         return int(m > 0) + int(m > 3)
@@ -507,7 +507,10 @@
         1,
     )
     refined = mm(wide_rows(mix_two[...]), tall(total)) + scalar_feat[:, 0:384]
+    for g in range(3):
+        mix_back[g] = wide_rows(mixing[g].T)
     hidden = mm(wide_rows(read_hidden[...]), tall(refined))
+    square_back[...] = wide_rows(square_mix[...].T)
     act, dact = silu_pair(hidden)
     out_column = jnp.broadcast_to(column_of(read_out[...])[:, 0:1], (16, 384))
     one_column = column_of(readout_one[...])
@@ -546,7 +549,7 @@
         grad = raw_ref[m % 3]
         if m == 0:
             grad = grad + refined_grad[:, 0:256] + jnp.concatenate([one_column] * 2, 1)
-            square_grad[...] = 2.0 * mm(wide_rows(square_mix[...].T), tall(grad))
+            square_grad[...] = 2.0 * mm(square_back[...], tall(grad))
         grad = mm(mix_back[degree(m)], tall(grad))
         grad_ref[m % 3] = grad + square_grad[...] * moments[m, :, 0:256]
 
@@ -583,22 +586,30 @@
     back_one = (jnp.concatenate(split(out_one[...]), 0), wide(mid_one[...]), wide(in_one[...].T))
     back_two = (jnp.concatenate(split(out_two[...]), 0), wide(mid_two[...]), wide(in_two[...].T))
 
-    def network_back(weights, grads, chunk, slot):
+    def out_back(weights, grads, chunk, slot):
         high, low = split(jnp.concatenate(grads, 0))
-        top_grad = mm(weights[0], high)
-        top_grad = top_grad[0:64] + top_grad[64:128] + mm(weights[0][0:64], low)
-        hid_grad = mm(weights[1], tall(top_grad * slopes[slot + 1, :, chunk]))
-        return mm(weights[2], tall(hid_grad * slopes[slot, :, chunk]))
-
-    parts = []
-    for start in range(0, EDGES_BACK, 256):
-        chunk = slice(start, start + 256)
+        value = mm(weights[0], high)
+        value = value[0:64] + value[64:128] + mm(weights[0][0:64], low)
+        stack[slot // 2, :, chunk] = tall(value * slopes[slot + 1, :, chunk])
+
+    parts = [slice(start, start + 256) for start in range(0, EDGES_BACK, 256)]
+    nets = ((back_one, 0), (back_two, 2))
+    for chunk in parts:
+        twos = [proj[g, :, chunk] for g in range(3)]
+        out_back(back_two, twos, chunk, 2)
         ones = [radial_grad[g, :, chunk] * emb_edge[:, chunk] for g in range(3)]
-        twos = [proj[g, :, chunk] for g in range(3)]
-        parts.append(
-            network_back(back_one, ones, chunk, 0) + network_back(back_two, twos, chunk, 2)
-        )
-    basis_grad = jnp.concatenate(parts, 1)
+        out_back(back_one, ones, chunk, 0)
+    for chunk in parts:
+        for weights, slot in nets:
+            value = mm(weights[1], stack[slot // 2, :, chunk])
+            stack[slot // 2, :, chunk] = tall(value * slopes[slot, :, chunk])
+    basis_grad = jnp.concatenate(
+        [
+            mm(back_one[2], stack[0, :, chunk]) + mm(back_two[2], stack[1, :, chunk])
+            for chunk in parts
+        ],
+        1,
+    )
 
     ux, uy, uz, inverse = ux[:, near], uy[:, near], uz[:, near], inverse[:, near]
     ym = [shape_grad[m : m + 1, :] for m in range(9)]
@@ -735,6 +746,7 @@
             pltpu.VMEM((3, 256, EDGES_TWO), BF16),
             pltpu.VMEM((3, 128, 256), F32),
             pltpu.VMEM((3, 128, 256), F32),
+            pltpu.VMEM((128, 384), BF16),
         ]
         + [pltpu.VMEM(h.shape, h.dtype) for h in held]
         + [pltpu.SemaphoreType.DMA((len(held),))],

time: 44.3 us -> 43.5 us (0.982)
  Pallas kernels: 14.9 us -> 14.1 us
    pallas_call x1, Pallas kernels: 13.4 us -> 12.6 us  [local(): pl.pallas_call(main_kernel, out_shape=(jax.ShapeDtypeStruct((3, 1, 128),...]
where the time goes in v3:
time: 43.5 us; the launch traced here: 42.9 us
  starting transfers between devices  23.3 us (54%)
  Pallas kernels  14.1 us (32%)
  waiting for transfers between devices  3.5 us (8%)
  local copies, waits for them, and re-layouts  1.29 us (3%)
  between operations  0.73 us (2%)
    ppermute x4, starting transfers between devices, swap(): return lax.ppermute(value, axis, pairs)  23.3 us
    pallas_call x1, Pallas kernels, local(): pl.pallas_call(main_kernel, out_shape=(jax.ShapeDtypeStruct((3, 1, 128),...  12.6 us
    ppermute x4, waiting for transfers between devices, swap(): return lax.ppermute(value, axis, pairs)  3.5 us
    pallas_call x1, Pallas kernels, local(): pl.pallas_call(pack_kernel, out_shape=jax.ShapeDtypeStruct((16, 128), F32...  1.49 us
    unnamed x8, local copies, waits for them, and re-layouts  1.29 us
  transfers between devices with their start and end apart: 4, of which 2 were waited for; matrix products, arithmetic and copies ran while one was open for 0% of the time, Pallas kernels for 0%

profile of v3, /device:TPU:1, one launch (start us, length us, event | category | flops | bytes accessed | tf_op | source)
XLA Modules:
  0.0 42.9 jit_solution(8350500465417354903)
XLA Ops:
  0.6 1.5 %shard_map.212 = f32[16,128]{1,0:T(8,128)} custom-call(f32[3,1,128]{2,1,0:T(1,128)} %bitcast.23, s32[1,128]{1,0:T(1,128)} %bitcast.28, s32[3,1,128]{2,1,0:T(1,128)} %bitcast.24, s32[1,128]{1,0:T(1,128)} %bitcast.29, s32[3,1,128]{2,1,0:T(1,128)} %bitcast.25, s32[1,64]{1,0:T(1,128)} %bitcast.30), custom_call_target="tpu_custom_call" | custom-call | tf_op jit(solution)/shard_map/pallas_call | solution.py:664
  2.1 4.6 %collective-permute-start.1 = (f32[16,128]{1,0:T(8,128)}, f32[16,128]{1,0:T(8,128)S(1)}, u32[]{:S(2)}, u32[]{:S(2)}) collective-permute-start(f32[16,128]{1,0:T(8,128)} %shard_map.212), channel_id=1, source_target_pairs={{0,15},{1,2},{2,1},{3,4},{4,3},{5,6},{6,5},{7,8},{8,7},{9,10},{10,... | collective-permute-start | bytes 24584 | tf_op jit(solution)/shard_map/ppermute | solution.py:640
  6.7 6.1 %collective-permute-start = (f32[16,128]{1,0:T(8,128)}, f32[16,128]{1,0:T(8,128)S(1)}, u32[]{:S(2)}, u32[]{:S(2)}) collective-permute-start(f32[16,128]{1,0:T(8,128)} %shard_map.212), channel_id=1, source_target_pairs={{0,1},{1,0},{2,3},{3,2},{4,5},{5,4},{6,7},{7,6},{8,9},{9,8},{10,11... | collective-permute-start | bytes 24584 | tf_op jit(solution)/shard_map/ppermute | solution.py:640
  12.8 0.0 collective-permute-done.1
  12.9 1.0 %collective-permute-done = f32[16,128]{1,0:T(8,128)S(1)} collective-permute-done((f32[16,128]{1,0:T(8,128)}, f32[16,128]{1,0:T(8,128)S(1)}, u32[]{:S(2)}, u32[]{:S(2)}) %collective-permute-start) | collective-permute-done | bytes 8224 | tf_op jit(solution)/shard_map/ppermute | solution.py:640
  13.8 0.0 copy-start.1
  13.8 0.7 %copy-done.1 = f32[16,128]{1,0:T(8,128)S(1)} copy-done((f32[16,128]{1,0:T(8,128)S(1)}, f32[16,128]{1,0:T(8,128)}, u32[]{:S(2)}) %copy-start.1) | copy-done | bytes 8216
  14.5 0.0 copy-start
  14.5 10.7 %collective-permute-start.3 = (f32[16,256]{1,0:T(8,128)S(1)}, f32[16,256]{1,0:T(8,128)S(1)}, u32[]{:S(2)}, u32[]{:S(2)}) collective-permute-start(f32[16,256]{1,0:T(8,128)S(1)} %pad_maximum_fusion.mid), channel_id=1, source_target_pairs={{0,496},{16,32},{32,16},{48,64},{64,48},{80,96},{96,80},{112,128},... | collective-permute-start | bytes 49160 | tf_op jit(solution)/shard_map/ppermute | solution.py:640
  25.2 1.9 %collective-permute-start.2 = (f32[16,256]{1,0:T(8,128)S(1)}, f32[16,256]{1,0:T(8,128)S(1)}, u32[]{:S(2)}, u32[]{:S(2)}) collective-permute-start(f32[16,256]{1,0:T(8,128)S(1)} %pad_maximum_fusion.mid), channel_id=1, source_target_pairs={{0,16},{16,0},{32,48},{48,32},{64,80},{80,64},{96,112},{112,96},{1... | collective-permute-start | bytes 49160 | tf_op jit(solution)/shard_map/ppermute | solution.py:640
  27.2 0.0 collective-permute-done.3.near_b
  27.2 0.0 copy-start.2
  27.2 2.5 %collective-permute-done.2.near_a = f32[16,256]{1,0:T(8,128)S(1)} collective-permute-done((f32[16,256]{1,0:T(8,128)S(1)}, f32[16,256]{1,0:T(8,128)S(1)}, u32[]{:S(2)}, u32[]{:S(2)}) %collective-permute-start.2) | collective-permute-done | bytes 16416 | tf_op jit(solution)/shard_map/ppermute | solution.py:640
  29.7 0.0 copy-start.3
  29.7 0.0 copy-done
  29.7 0.0 copy-done.2
  29.7 0.6 %copy-done.3 = f32[16,256]{1,0:T(8,128)} copy-done((f32[16,256]{1,0:T(8,128)}, f32[16,256]{1,0:T(8,128)S(1)}, u32[]{:S(2)}) %copy-start.3) | copy-done | bytes 16408
  30.3 12.6 %shard_map.213 = (f32[3,1,128]{2,1,0:T(1,128)}, f32[1,128]{1,0:T(1,128)}) custom-call(s32[1]{0:T(128)} %bitcast.odd, f32[16,256]{1,0:T(8,128)} %copy-done, f32[16,256]{1,0:T(8,128)} %copy-done.3, f32[16,256]{1,0:T(8,128)} %copy-done.2, s32[8,512]{1,0:T(8,128)} %constant.56.clone.atom_table_hbm, s32[8,1408]{1,0:T(8,128)} %constant.57.clone.edge_table_hbm, ...), custom_call_target="tpu_custom_call" | custom-call | tf_op jit(solution)/shard_map/pallas_call | solution.py:712
  (4 shorter events, 0.0 us)
Async XLA Ops:
  2.1 10.7 %collective-permute-start.1 = (f32[16,128]{1,0:T(8,128)}, f32[16,128]{1,0:T(8,128)S(1)}, u32[]{:S(2)}, u32[]{:S(2)}) collective-permute-start(f32[16,128]{1,0:T(8,128)} %shard_map.212), channel_id=1, source_target_pairs={{0,15},{1,2},{2,1},{3,4},{4,3},{5,6},{6,5},{7,8},{8,7},{9,10},{10,... | collective-permute-start | bytes 24584 | tf_op jit(solution)/shard_map/ppermute | solution.py:640
  6.7 7.1 %collective-permute-start = (f32[16,128]{1,0:T(8,128)}, f32[16,128]{1,0:T(8,128)S(1)}, u32[]{:S(2)}, u32[]{:S(2)}) collective-permute-start(f32[16,128]{1,0:T(8,128)} %shard_map.212), channel_id=1, source_target_pairs={{0,1},{1,0},{2,3},{3,2},{4,5},{5,4},{6,7},{7,6},{8,9},{9,8},{10,11... | collective-permute-start | bytes 24584 | tf_op jit(solution)/shard_map/ppermute | solution.py:640
  13.8 0.7 %copy-start.1 = (f32[16,128]{1,0:T(8,128)S(1)}, f32[16,128]{1,0:T(8,128)}, u32[]{:S(2)}) copy-start(f32[16,128]{1,0:T(8,128)} %shard_map.212) | copy-start | bytes 24580
  14.5 15.2 %copy-start = (f32[16,256]{1,0:T(8,128)}, f32[16,256]{1,0:T(8,128)S(1)}, u32[]{:S(2)}) copy-start(f32[16,256]{1,0:T(8,128)S(1)} %pad_maximum_fusion.mid) | copy-start | bytes 49156
  14.5 12.6 %collective-permute-start.3 = (f32[16,256]{1,0:T(8,128)S(1)}, f32[16,256]{1,0:T(8,128)S(1)}, u32[]{:S(2)}, u32[]{:S(2)}) collective-permute-start(f32[16,256]{1,0:T(8,128)S(1)} %pad_maximum_fusion.mid), channel_id=1, source_target_pairs={{0,496},{16,32},{32,16},{48,64},{64,48},{80,96},{96,80},{112,128},... | collective-permute-start | bytes 49160 | tf_op jit(solution)/shard_map/ppermute | solution.py:640
  25.2 4.5 %collective-permute-start.2 = (f32[16,256]{1,0:T(8,128)S(1)}, f32[16,256]{1,0:T(8,128)S(1)}, u32[]{:S(2)}, u32[]{:S(2)}) collective-permute-start(f32[16,256]{1,0:T(8,128)S(1)} %pad_maximum_fusion.mid), channel_id=1, source_target_pairs={{0,16},{16,0},{32,48},{48,32},{64,80},{80,64},{96,112},{112,96},{1... | collective-permute-start | bytes 49160 | tf_op jit(solution)/shard_map/ppermute | solution.py:640
  27.2 2.5 %copy-start.2 = (f32[16,256]{1,0:T(8,128)}, f32[16,256]{1,0:T(8,128)S(1)}, u32[]{:S(2)}) copy-start(f32[16,256]{1,0:T(8,128)S(1)} %collective-permute-done.3.near_b) | copy-start | bytes 49156
  29.7 0.6 %copy-start.3 = (f32[16,256]{1,0:T(8,128)}, f32[16,256]{1,0:T(8,128)S(1)}, u32[]{:S(2)}) copy-start(f32[16,256]{1,0:T(8,128)S(1)} %collective-permute-done.2.near_a) | copy-start | bytes 49156
